TPU v7x, 256 devices: a whole 4x4x8 slice. The times are simulated.
256 devices in a mesh: row: 8 (over x, z_lo), col: 32 (over y, z_hi, core).
Axes of the slice: x: 4, y: 4, z: 8 (z_hi: 4, z_lo: 2; z = z_hi * 2 + z_lo), core: 2. Of those that a mesh axis runs over, the one named last changes fastest.
Arguments:
- hamiltonian: float32 [4096, 4096], P('row', 'col'), as said below
- h_mask: int32 [32, 32], P('row', 'col'), may hold values from 0 to 1, as said below
- factor: float32 [4096, 4096], P('row', 'col'), may hold values from -0.125 to 0.125
- z_mask: int32 [32, 32], P('row', 'col'), may hold values 0 or 1
- k_mask: int32 [32, 32], P('row', 'col'), may hold values 0 or 1
- block_sizes: int32 [32], replicated, may hold values from 64 to 128, as said below
Outputs:
- transformed: float32 [4096, 4096], P('row', 'col')
Inputs may be any that keep to these rules, and one draw needn't show every extreme that they name: hamiltonian is symmetric. `h_mask`: symmetric, with every diagonal block occupied. `block_sizes`: some block uses all 128 orbitals.
All inputs are finite; a program needn't handle non-finite values. No bound on the sum of `z_mask` or of `k_mask` on one device may be relied on, other than what follows from the above.
Results may differ from a plain program's by a relative error of at most 0.000098.
Values sent between devices are 32-bit elements; how exact they have to be, the bound alone decides.
A program may use at most 64 MiB of HBM per device.

v0:
```python
import jax
import jax.numpy as jnp
from jax import lax
from jax.sharding import PartitionSpec as P

BLOCK = 128


def expand(blocks):
    grown = jnp.repeat(blocks.astype(jnp.float32), BLOCK, axis=0)
    return jnp.repeat(grown, BLOCK, axis=1)


def validity(block_sizes, first, count):
    sizes = lax.dynamic_slice_in_dim(block_sizes, first, count, 0)
    within = jnp.arange(BLOCK, dtype=jnp.int32)
    return (within[None, :] < sizes[:, None]).astype(jnp.float32).reshape(-1)


def local(hamiltonian, h_mask, factor, z_mask, k_mask, block_sizes):
    rows_here, cols_here = hamiltonian.shape
    row_blocks = rows_here // BLOCK
    col_blocks = cols_here // BLOCK
    row_place = lax.axis_index("row")
    row_first = row_place * row_blocks
    col_first = lax.axis_index("col") * col_blocks
    row_valid = validity(block_sizes, row_first, row_blocks)
    col_valid = validity(block_sizes, col_first, col_blocks)
    outer = row_valid[:, None] * col_valid[None, :]
    global_rows = row_first * BLOCK + jnp.arange(rows_here, dtype=jnp.int32)
    global_cols = col_first * BLOCK + jnp.arange(cols_here, dtype=jnp.int32)
    upper = (global_rows[:, None] <= global_cols[None, :]).astype(jnp.float32)
    hmat = hamiltonian * expand(h_mask) * outer
    zmat = factor * expand(z_mask) * outer * upper
    highest = lax.Precision.HIGHEST
    zcolumn = lax.all_gather(zmat, "row", axis=0, tiled=True)
    hz_tile = jnp.dot(
        lax.all_gather(hmat, "col", axis=1, tiled=True),
        zcolumn,
        precision=highest,
        preferred_element_type=jnp.float32,
    )
    terms = jnp.dot(
        lax.all_gather(zmat, "col", axis=1, tiled=True).T,
        hz_tile,
        precision=highest,
        preferred_element_type=jnp.float32,
    )
    result = lax.psum_scatter(terms, "row", scatter_dimension=0, tiled=True)
    return result * expand(k_mask)


def solution(mesh):
    placed = (
        P("row", "col"),
        P("row", "col"),
        P("row", "col"),
        P("row", "col"),
        P("row", "col"),
        P(),
    )
    return jax.shard_map(
        local, mesh=mesh, in_specs=placed, out_specs=P("row", "col"), check_vma=False
    )
```

profile of v0, /device:TPU:34, one launch (start us, length us, event | category | flops | bytes accessed | tf_op | source)
XLA Modules:
  0.0 320.3 jit_solution(6343206805627346707)
XLA Ops:
  6.5 0.7 dynamic_slice.6
  7.3 0.1 convert_bitcast_fusion
  7.3 1.2 dynamic_slice.7
  8.6 0.6 compare_convert_fusion
  9.3 0.7 convert_bitcast_fusion.2
  9.9 0.7 convert_bitcast_fusion.3
  10.6 0.1 broadcast_bitcast_fusion.1
  10.7 2.1 multiply_multiply_fusion
  12.8 0.0 all-gather.8.cloned.1.call-update
  12.8 0.0 all-gather.6.cloned.1.call-start
  12.9 0.7 all-gather.6.cloned.1.call-update
  13.6 0.0 all-gather.4.cloned.1.call-start
  13.6 0.7 all-gather.4.cloned.1.call-update
  14.3 0.0 reduce-scatter.2.cloned.1.call-start
  14.3 54.0 %all-gather.8.cloned.1.call-done = f32[4096,128]{1,0:T(8,128)} async-done(((f32[512,128]{1,0:T(8,128)}), f32[4096,128]{1,0:T(8,128)}) %all-gather.8.cloned.1.call-update) | async-done | bytes 2097168 | tf_op jit(solution)/shard_map/all_gather | solution.py:36
  68.4 86.7 %all-gather.6.cloned.1.call-done = f32[512,4096]{1,0:T(8,128)} async-done(((f32[512,128]{1,0:T(8,128)}), f32[512,4096]{1,0:T(8,128)}) %all-gather.6.cloned.1.call-update) | async-done | bytes 8388624 | tf_op jit(solution)/shard_map/all_gather | solution.py:38
  155.1 9.3 %fusion.1 = f32[512,128]{1,0:T(8,128)S(1)} fusion(f32[512,4096]{1,0:T(8,128)} %all-gather.6.cloned.1.call-done, f32[4096,128]{1,0:T(8,128)} %all-gather.8.cloned.1.call-done), kind=kOutput, calls=%fused_computation.15 | convolution fusion | flops 3221225472 | bytes 10747904 | tf_op jit(solution)/shard_map/dot_general | solution.py:37
  164.5 0.0 copy-start
  164.5 76.9 %all-gather.4.cloned.1.call-done = f32[512,4096]{1,0:T(8,128)} async-done(((f32[512,128]{1,0:T(8,128)}), f32[512,4096]{1,0:T(8,128)}) %all-gather.4.cloned.1.call-update) | async-done | bytes 8388624 | tf_op jit(solution)/shard_map/all_gather | solution.py:44
  241.4 16.5 %fusion.2 = f32[4096,128]{1,0:T(8,128)} fusion(f32[512,4096]{1,0:T(8,128)} %all-gather.4.cloned.1.call-done, f32[512,128]{1,0:T(8,128)S(1)} %fusion.1), kind=kOutput, calls=%fused_computation.16 | convolution fusion | flops 3221225472 | bytes 10747904 | tf_op jit(solution)/shard_map/dot_general | solution.py:43
  257.9 0.0 reduce-scatter.2.cloned.1.call-update
  258.0 0.1 broadcast_bitcast_fusion
  258.1 54.0 %reduce-scatter.2.cloned.1.call-done = f32[512,128]{1,0:T(8,128)} async-done(((f32[4096,128]{1,0:T(8,128)}), f32[512,128]{1,0:T(8,128)}) %reduce-scatter.2.cloned.1.call-update) | async-done | bytes 262160 | tf_op jit(solution)/shard_map/reduce_scatter | solution.py:49
  312.0 1.8 broadcast_multiply_fusion
  (5 shorter events, 0.0 us)
Async XLA Ops:
  6.5 61.9 %all-gather.8.cloned.1.call-start = ((), (), s32[]{:S(2)}) async-start(), calls=%async_computation.3 | async-start | bytes 2359296 | tf_op jit(solution)/shard_map/all_gather | solution.py:36
  12.8 142.3 %all-gather.6.cloned.1.call-start = ((), (), s32[]{:S(2)}) async-start(), calls=%async_computation.2 | async-start | bytes 8650752 | tf_op jit(solution)/shard_map/all_gather | solution.py:38
  13.6 227.8 %all-gather.4.cloned.1.call-start = ((), (), s32[]{:S(2)}) async-start(), calls=%async_computation.1 | async-start | bytes 8650752 | tf_op jit(solution)/shard_map/all_gather | solution.py:44
  14.3 297.7 %reduce-scatter.2.cloned.1.call-start = ((), (), s32[]{:S(2)}) async-start(), calls=%async_computation.4 | async-start | bytes 2359296 | tf_op jit(solution)/shard_map/reduce_scatter | solution.py:49
  164.5 93.5 %copy-start = (s32[4,1]{0,1:T(1,128)S(1)}, s32[4,1]{0,1:T(1,128)}, u32[]{:S(2)}) copy-start(s32[4,1]{0,1:T(1,128)} %param.10) | copy-start | bytes 52
Sparse Core Ops, SparseCore 0:
  12.9 55.4 all-gather.7
  70.9 84.1 all-gather.5
  157.6 83.7 all-gather.3
  258.1 53.8 reduce-scatter.1
where the time goes:
time: 323 us; the launch traced here: 320 us
  waiting for transfers between devices  273 us (85%)
  matrix products  25.9 us (8%)
  between operations  13.2 us (4%)
  other arithmetic  5.97 us (2%)
    all_gather x1, waiting for transfers between devices, local(): lax.all_gather(hmat, 'col', axis=1, tiled=True)  86.7 us
    all_gather x1, waiting for transfers between devices, local(): lax.all_gather(zmat, 'col', axis=1, tiled=True)  76.9 us
    all_gather x1, waiting for transfers between devices, local(): zcolumn = lax.all_gather(zmat, 'row', axis=0, tiled=True)  54 us
    reduce_scatter x1, waiting for transfers between devices, local(): result = lax.psum_scatter(terms, 'row', scatter_dimension=0, tiled=True)  54 us
    dot_general x1, matrix products, local(): jnp.dot(lax.all_gather(zmat, 'col', axis=1, tiled=True).T, hz_tile, preci...  16.5 us
    dot_general x1, matrix products, local(): jnp.dot(lax.all_gather(hmat, 'col', axis=1, tiled=True), zcolumn, precisi...  9.35 us
  transfers between devices with their start and end apart: 4, of which 4 were waited for; matrix products, arithmetic and copies ran while one was open for 3% of the time, Pallas kernels for 0%

commit v1 on v0

v1 whole, which is shorter than its diff:
```python
import jax
import jax.numpy as jnp
from jax import lax
from jax.experimental import pallas as pl
from jax.experimental.pallas import tpu as pltpu
from jax.sharding import PartitionSpec as P

B = 128
MESH = pl.DeviceIdType.MESH
ORDER = (0, 2, 1, 3)
F32 = jnp.float32


def split(v):
    hi = v.astype(jnp.bfloat16)
    return hi, (v - hi.astype(F32)).astype(jnp.bfloat16)


def dot(a, b):
    return jnp.dot(a, b, preferred_element_type=F32)


def dot3(ah, al, bh, bl):
    return dot(ah, bh) + (dot(ah, bl) + dot(al, bh))


def kernel(h_ref, hm_ref, z_ref, zm_ref, km_ref, size_ref, out_ref,
           hg, zg, sw, xg, z1, z1h, z1l, wp, cr, wc, yr, wt, wh, wl, u, xr, fin, tr,
           h_ss, h_rs, z_ss, z_rs, sw_s, ce_s, xa_ss, xa_rs, ya_ss, ya_rs,
           wc_ss, wc_rs, wy_ss, wy_rs, wa_ss, wa_rs, wf_ss, wf_rs, ux_ss, ux_rs, fd_ss, fd_rs):
    row = lax.axis_index("row")
    col = lax.axis_index("col")
    x, zl = row // 2, row % 2
    y, zh, c = col // 8, (col // 2) % 4, col % 2
    z = zh * 2 + zl

    def dev(x_, y_, z_, c_):
        return (x_ * 2 + z_ % 2, (y_ * 4 + z_ // 2) * 2 + c_)

    def remote(src, dst, ss, rs, to):
        return pltpu.make_async_remote_copy(
            src_ref=src, dst_ref=dst, send_sem=ss, recv_sem=rs, device_id=to, device_id_type=MESH)

    sib = dev(x, y, z, 1 - c)
    xpeer = [None] + [dev((x + d) % 4, y, z, c) for d in (1, 2, 3)]
    ypeer = [None] + [dev(x, (y + d) % 4, z, c) for d in (1, 2, 3)]
    zpeer = [dev(x, y, (z + 1) % 8, c), dev(x, y, (z + 7) % 8, c)]
    partner = dev(x, y, zh * 2 + c, zl)
    crossed = zl != c
    homed = zl == zh // 2

    barrier = pltpu.get_barrier_semaphore()
    for to in [sib] + xpeer[1:] + ypeer[1:] + zpeer:
        pl.semaphore_signal(barrier, inc=1, device_id=to, device_id_type=MESH)

    @pl.when(crossed)
    def _():
        pl.semaphore_signal(barrier, inc=1, device_id=partner, device_id_type=MESH)

    for b in range(4):
        @pl.when(zl * 4 + b != z)
        def _():
            pl.semaphore_signal(barrier, inc=1, device_id=dev(x, y, zl * 4 + b, c), device_id_type=MESH)

    ri = lax.broadcasted_iota(jnp.int32, (B, B), 0)
    ci = lax.broadcasted_iota(jnp.int32, (B, B), 1)
    colok = ci < size_ref[col]
    for s, b in enumerate(ORDER):
        rb = row * 4 + b
        ok = jnp.logical_and(colok, ri < size_ref[rb]).astype(F32)
        hg[z, s * B:(s + 1) * B, :] = h_ref[b * B:(b + 1) * B, :] * (ok * hm_ref[b, 0].astype(F32))
        up = (ri + rb * B <= ci + col * B).astype(F32)
        zg[z, s * B:(s + 1) * B, :] = z_ref[b * B:(b + 1) * B, :] * (ok * up * zm_ref[b, 0].astype(F32))

    pl.semaphore_wait(barrier, 13 + crossed.astype(jnp.int32) - homed.astype(jnp.int32))

    def ring(buf, ss, rs):
        made = {}

        def step(st, subs):
            for s in subs:
                for d in range(2):
                    if st > 0:
                        made[st - 1, s, d].wait_recv()
                    if st == 3 and s % 2 != d:
                        continue
                    slot = (z + 8 - st) % 8 if d == 0 else (z + st) % 8
                    part = buf.at[slot, pl.ds(s * B, B)]
                    cp = remote(part, part, ss.at[d, st, s], rs.at[d, st, s], zpeer[d])
                    cp.start()
                    made[st, s, d] = cp

        def last(subs):
            for s in subs:
                made[3, s, s % 2].wait_recv()

        def sent():
            for cp in made.values():
                cp.wait_send()

        return step, last, sent

    hstep, hlast, hsent = ring(hg, h_ss, h_rs)
    zstep, zlast, zsent = ring(zg, z_ss, z_rs)

    hstep(0, (0, 1))

    swap = remote(zg.at[z], sw, sw_s.at[0], sw_s.at[1], partner)

    @pl.when(crossed)
    def _():
        swap.start()

    @pl.when(jnp.logical_not(crossed))
    def _():
        sw[...] = zg[z]

    @pl.when(crossed)
    def _():
        swap.wait_recv()

    mine = pl.ds(pl.multiple_of(c * 256, 256), 256)
    other = pl.ds(pl.multiple_of((1 - c) * 256, 256), 256)
    cex = remote(sw.at[other], xg.at[x, mine], ce_s.at[0], ce_s.at[1], sib)
    cex.start()
    xg[x, mine, :] = sw[mine, :]
    hstep(1, (0, 1))
    cex.wait_recv()
    xa = {}
    for d in (1, 3, 2):
        xa[d] = remote(xg.at[x], xg.at[x], xa_ss.at[d], xa_rs.at[d], xpeer[d])
        xa[d].start()
    ya = {}

    def ysend(e):
        src = (x + 4 - e) % 4
        d = (src + 4 - y) % 4
        ya[e] = d, remote(xg.at[src], z1.at[y], ya_ss.at[e], ya_rs.at[d], dev(x, src, z, c))

        @pl.when(d != 0)
        def _():
            ya[e][1].start()

    ysend(0)
    hstep(2, (0, 1))
    for e in (1, 3):
        xa[e].wait_recv()
        ysend(e)
    hstep(3, (0, 1))
    hstep(0, (2, 3))
    xa[2].wait_recv()
    ysend(2)
    z1[y] = xg[y]
    hlast((0, 1))
    hstep(1, (2, 3))
    for d in (1, 2, 3):
        remote(xg.at[0], z1.at[y], ya_ss.at[0], ya_rs.at[d], sib).wait_recv()
    for j in range(4):
        hi, lo = split(z1[j])
        z1h[:, j * B:(j + 1) * B] = hi
        z1l[:, j * B:(j + 1) * B] = lo

    def first(k):
        rows = slice(k * 256, (k + 1) * 256)
        for half in range(2):
            a = jnp.concatenate([hg[2 * q + half, rows, :] for q in range(4)], axis=1)
            ah, al = split(a)
            wp[k, half * 256:(half + 1) * 256, :] = dot3(ah, al, z1h[...], z1l[...])
        cp = remote(wp.at[k, other], cr.at[k], wc_ss.at[k], wc_rs.at[k], sib)
        cp.start()
        return cp

    def scatter(k, cp):
        cp.wait_recv()
        tot = wp[k, mine, :] + cr[k]
        for q in range(4):
            wc[k, q] = tot[:, q * B:(q + 1) * B]
        cps = {}
        for d in (1, 3, 2):
            cps[d] = remote(wc.at[k, (y + d) % 4], yr.at[k, d - 1], wy_ss.at[k, d], wy_rs.at[k, d], ypeer[d])
            cps[d].start()
        return cps

    def spread(k, cps):
        for d in (1, 3, 2):
            cps[d].wait_recv()
        r = (wc[k, y] + yr[k, 0]) + (yr[k, 1] + yr[k, 2])
        wt[k, y, c] = r.T
        own = wt.at[k, y, c]
        out = {}
        for d in (1, 3, 2):
            out[d] = remote(own, own, wa_ss.at[k, d], wa_rs.at[k, d], ypeer[d])
            out[d].start()
        out[0] = remote(own, own, wf_ss.at[k, 0], wf_rs.at[k, 0], sib)
        out[0].start()
        return out

    def forward(k, out):
        fw = {}
        for d in (1, 3, 2):
            out[d].wait_recv()
            part = wt.at[k, (y + 4 - d) % 4, c]
            fw[d] = remote(part, part, wf_ss.at[k, d], wf_rs.at[k, d], sib)
            fw[d].start()
        return fw

    def gathered(k, out, fw):
        out[0].wait_recv()
        for d in (1, 3, 2):
            fw[d].wait_recv()
        for q in range(4):
            for half in range(2):
                hi, lo = split(wt[k, q, half])
                at = (k * 2 + half) * 256
                wh[q * B:(q + 1) * B, at:at + 256] = hi
                wl[q * B:(q + 1) * B, at:at + 256] = lo

    c0 = first(0)
    hstep(2, (2, 3))
    s0 = scatter(0, c0)
    hstep(3, (2, 3))
    zstep(0, (0, 1, 2, 3))
    o0 = spread(0, s0)
    hlast((2, 3))
    c1 = first(1)
    f0 = forward(0, o0)
    s1 = scatter(1, c1)
    zstep(1, (0, 1, 2, 3))
    gathered(0, o0, f0)
    o1 = spread(1, s1)
    f1 = forward(1, o1)
    gathered(1, o1, f1)

    shift = zl * 2 + 3
    near = [zh, (zh + shift) % 4, (zh + 4 - shift % 4) % 4, (zh + 2) % 4]

    def second(j):
        zz = near[j]
        b = jnp.concatenate(
            [zg[zz * 2 + half, k * 256:(k + 1) * 256, :] for k in range(2) for half in range(2)], axis=0)
        bh, bl = split(b)
        t = dot3(wh[...], wl[...], bh, bl)
        for q in range(4):
            u[j, q] = t[q * B:(q + 1) * B, :]
        cps = {}
        for d in (1, 3, 2):
            cps[d] = remote(u.at[j, (x + d) % 4], xr.at[j, d - 1], ux_ss.at[j, d], ux_rs.at[j, d], xpeer[d])
            cps[d].start()
        return cps

    place = (zh % 2) * 2 + zl
    away = [None] * 4

    def deliver(j, cps):
        for d in (1, 3, 2):
            cps[d].wait_recv()
        v = (u[j, x] + xr[j, 0]) + (xr[j, 1] + xr[j, 2])
        fin[j] = v
        away[j] = remote(fin.at[j], tr.at[place], fd_ss.at[j], fd_rs.at[place],
                         dev(x, y, near[j] * 2 + zh // 2, c))
        if j == 0:
            @pl.when(homed)
            def _():
                tr[place] = fin[0]

            @pl.when(jnp.logical_not(homed))
            def _():
                away[0].start()
        else:
            away[j].start()

    u0 = second(0)
    zstep(2, (0, 1, 2, 3))
    u1 = second(1)
    deliver(0, u0)
    zstep(3, (0, 1, 2, 3))
    u2 = second(2)
    deliver(1, u1)
    zlast((0, 1, 2, 3))
    u3 = second(3)
    deliver(2, u2)
    deliver(3, u3)
    for b in range(4):
        @pl.when(zl * 4 + b != z)
        def _():
            remote(fin.at[0], tr.at[b], fd_ss.at[0], fd_rs.at[b], sib).wait_recv()

        out_ref[b * B:(b + 1) * B, :] = tr[b] * km_ref[b, 0].astype(F32)

    hsent()
    zsent()

    @pl.when(crossed)
    def _():
        swap.wait_send()

    cex.wait_send()
    for d in (1, 2, 3):
        xa[d].wait_send()
    for e in range(4):
        @pl.when(ya[e][0] != 0)
        def _():
            ya[e][1].wait_send()
    for group in (s0, s1, o0, o1, f0, f1, u0, u1, u2, u3):
        for cp in group.values():
            cp.wait_send()
    c0.wait_send()
    c1.wait_send()

    @pl.when(jnp.logical_not(homed))
    def _():
        away[0].wait_send()

    for j in (1, 2, 3):
        away[j].wait_send()


def local(hamiltonian, h_mask, factor, z_mask, k_mask, block_sizes):
    vm = pl.BlockSpec(memory_space=pltpu.VMEM)
    sm = pl.BlockSpec(memory_space=pltpu.SMEM)
    dma = pltpu.SemaphoreType.DMA
    bf = jnp.bfloat16
    scratch = [
        pltpu.VMEM((8, 512, B), F32),
        pltpu.VMEM((8, 512, B), F32),
        pltpu.VMEM((512, B), F32),
        pltpu.VMEM((4, 512, B), F32),
        pltpu.VMEM((4, 512, B), F32),
        pltpu.VMEM((512, 512), bf),
        pltpu.VMEM((512, 512), bf),
        pltpu.VMEM((2, 512, 512), F32),
        pltpu.VMEM((2, 256, 512), F32),
        pltpu.VMEM((2, 4, 256, B), F32),
        pltpu.VMEM((2, 3, 256, B), F32),
        pltpu.VMEM((2, 4, 2, B, 256), F32),
        pltpu.VMEM((512, 1024), bf),
        pltpu.VMEM((512, 1024), bf),
        pltpu.VMEM((4, 4, B, B), F32),
        pltpu.VMEM((4, 3, B, B), F32),
        pltpu.VMEM((4, B, B), F32),
        pltpu.VMEM((4, B, B), F32),
        dma((2, 4, 4)), dma((2, 4, 4)), dma((2, 4, 4)), dma((2, 4, 4)),
        dma((2,)), dma((2,)), dma((4,)), dma((4,)), dma((4,)), dma((4,)),
        dma((2,)), dma((2,)), dma((2, 4)), dma((2, 4)), dma((2, 4)), dma((2, 4)),
        dma((2, 4)), dma((2, 4)), dma((4, 4)), dma((4, 4)), dma((4,)), dma((4,)),
    ]
    return pl.pallas_call(
        kernel,
        out_shape=jax.ShapeDtypeStruct((512, B), F32),
        in_specs=[vm, sm, vm, sm, sm, sm],
        out_specs=vm,
        scratch_shapes=scratch,
        compiler_params=pltpu.CompilerParams(
            collective_id=0, has_side_effects=True, vmem_limit_bytes=48 << 20),
        name="congruence",
    )(hamiltonian, h_mask, factor, z_mask, k_mask, block_sizes)


def solution(mesh):
    placed = (
        P("row", "col"),
        P("row", "col"),
        P("row", "col"),
        P("row", "col"),
        P("row", "col"),
        P(),
    )
    return jax.shard_map(
        local, mesh=mesh, in_specs=placed, out_specs=P("row", "col"), check_vma=False
    )
```

time: 323 us -> 119 us (0.37)
  waiting for transfers between devices: 273 us -> 0 us
  Pallas kernels: 0 us -> 113 us
  matrix products: 25.9 us -> 0 us
  between operations: 13.2 us -> 0.02 us
  other arithmetic: 5.97 us -> 0 us
    all_gather x3 -> x0, waiting for transfers between devices: 218 us -> none  [the longest x1 86.7 us: local(): lax.all_gather(hmat, 'col', axis=1, tiled=True)]
    pallas_call x0 -> x1, Pallas kernels: none -> 113 us  [local(): pl.pallas_call(kernel, out_shape=jax.ShapeDtypeStruct((512, B), F32), in_...]
    reduce_scatter x1 -> x0, waiting for transfers between devices: 54 us -> none  [local(): result = lax.psum_scatter(terms, 'row', scatter_dimension=0, tiled=True)]
    dot_general x2 -> x0, matrix products: 25.9 us -> none  [the longest x1 16.5 us: local(): jnp.dot(lax.all_gather(zmat, 'col', axis=1, tiled=True).T, hz_tile, preci...]
    unnamed x2 -> x14, local copies, waits for them, and re-layouts: 0.01 us -> 4.67 us
    mul x2 -> x0, other arithmetic: 3.92 us -> none  [the longest x1 2.13 us: local(): hmat = hamiltonian * expand(h_mask) * outer]
  transfers between devices with their start and end apart: 4 -> 0, of which waited for: 4 -> 0; matrix products, arithmetic and copies ran while one was open for 3% -> 0% of each run, Pallas kernels for 0% -> 0%
where the time goes in v1:
time: 119 us; the launch traced here: 118 us
  Pallas kernels  113 us (95%)
  local copies, waits for them, and re-layouts  4.67 us (4%)
    pallas_call x1, Pallas kernels, local(): pl.pallas_call(kernel, out_shape=jax.ShapeDtypeStruct((512, B), F32), in_...  113 us
    unnamed x14, local copies, waits for them, and re-layouts  4.67 us

profile of v1, /device:TPU:34, one launch (start us, length us, event | category | flops | bytes accessed | tf_op | source)
XLA Modules:
  0.0 117.7 jit_solution(12002057204252399950)
XLA Ops:
  0.0 0.0 copy-start.3
  0.0 0.8 copy.7.hm_ref
  0.8 0.0 copy-done.3
  0.8 0.0 copy-start.4
  0.8 0.1 copy.8.zm_ref
  0.9 0.6 copy-done.4
  1.4 0.0 copy-start.2
  1.4 0.1 copy.9.km_ref
  1.5 0.6 copy-done.2
  2.1 0.0 copy-start
  2.1 0.9 copy-done
  3.0 0.0 copy-start.1
  3.0 0.9 copy-done.1
  4.0 113.0 %congruence.1 = f32[512,128]{1,0:T(8,128)S(1)} custom-call(f32[512,128]{1,0:T(8,128)S(1)} %copy-done, s32[4,1]{1,0:T(4,128)S(1)} %copy.7.hm_ref, f32[512,128]{1,0:T(8,128)S(1)} %copy-done.1, s32[4,1]{1,0:T(4,128)S(1)} %copy.8.zm_ref, s32[4,1]{1,0:T(4,128)S(1)} %copy.9.km_ref, s32[32]{0:T(128)S(1)} %copy-done.2), custom_call_target="tpu_custom_call" | custom-call | tf_op jit(solution)/shard_map/congruence/pallas_call | solution.py:347
  117.0 0.7 copy.11
Async XLA Ops:
  0.0 0.8 copy-start.3
  0.8 0.7 copy-start.4
  1.4 0.7 copy-start.2
  2.1 0.9 copy-start
  3.0 0.9 copy-start.1

commit v2 on v1

v2 whole, which is shorter than its diff:
```python
import jax
import jax.numpy as jnp
from jax import lax
from jax.experimental import pallas as pl
from jax.experimental.pallas import tpu as pltpu
from jax.sharding import PartitionSpec as P

B = 128
MESH = pl.DeviceIdType.MESH
ORDER = (0, 2, 1, 3)
F32 = jnp.float32
CHUNKS = 2
HALF = B // CHUNKS


def split(v):
    hi = v.astype(jnp.bfloat16)
    return hi, (v - hi.astype(F32)).astype(jnp.bfloat16)


def dot3(ah, al, bh, bl):
    return jnp.dot(jnp.concatenate([ah, ah, al], axis=1), jnp.concatenate([bh, bl, bh], axis=0),
                   preferred_element_type=F32)


def kernel(h_hbm, hm_hbm, z_hbm, zm_hbm, km_hbm, size_hbm, out_ref,
           h_ref, z_ref, hm_ref, zm_ref, km_ref, size_ref, in_s,
           hg, zg, ah, al, bh, bl, sw, xg, z1, z1h, z1l, wp, cr, wc, yr, wt, u, xr, fin, tr,
           h_ss, h_rs, z_ss, z_rs, sw_s, ce_s, xa_ss, xa_rs, ya_ss, ya_rs,
           wc_ss, wc_rs, wy_ss, wy_rs, wa_ss, wa_rs, wf_ss, wf_rs, ux_ss, ux_rs, fd_ss, fd_rs):
    row = lax.axis_index("row")
    col = lax.axis_index("col")
    x, zl = row // 2, row % 2
    y, zh, c = col // 8, (col // 2) % 4, col % 2
    z = zh * 2 + zl

    loads = [
        pltpu.make_async_copy(src, dst, in_s.at[i])
        for i, (src, dst) in enumerate([
            (size_hbm, size_ref), (zm_hbm, zm_ref), (z_hbm, z_ref), (hm_hbm, hm_ref), (h_hbm, h_ref), (km_hbm, km_ref)])
    ]
    for cp in loads:
        cp.start()

    def dev(x_, y_, z_, c_):
        return (x_ * 2 + z_ % 2, (y_ * 4 + z_ // 2) * 2 + c_)

    def remote(src, dst, ss, rs, to):
        return pltpu.make_async_remote_copy(
            src_ref=src, dst_ref=dst, send_sem=ss, recv_sem=rs, device_id=to, device_id_type=MESH)

    sib = dev(x, y, z, 1 - c)
    xpeer = [None] + [dev((x + d) % 4, y, z, c) for d in (1, 2, 3)]
    ypeer = [None] + [dev(x, (y + d) % 4, z, c) for d in (1, 2, 3)]
    zpeer = [dev(x, y, (z + 1) % 8, c), dev(x, y, (z + 7) % 8, c)]
    partner = dev(x, y, zh * 2 + c, zl)
    crossed = zl != c
    homed = zl == zh // 2

    barrier = pltpu.get_barrier_semaphore()
    for to in [sib] + xpeer[1:] + ypeer[1:] + zpeer:
        pl.semaphore_signal(barrier, inc=1, device_id=to, device_id_type=MESH)

    @pl.when(crossed)
    def _():
        pl.semaphore_signal(barrier, inc=1, device_id=partner, device_id_type=MESH)

    for b in range(4):
        @pl.when(zl * 4 + b != z)
        def _():
            pl.semaphore_signal(barrier, inc=1, device_id=dev(x, y, zl * 4 + b, c), device_id_type=MESH)

    for cp in loads:
        cp.wait()
    ri = lax.broadcasted_iota(jnp.int32, (B, B), 0)
    ci = lax.broadcasted_iota(jnp.int32, (B, B), 1)
    colok = ci < size_ref[col]
    for s, b in enumerate(ORDER):
        rb = row * 4 + b
        ok = jnp.logical_and(colok, ri < size_ref[rb]).astype(F32)
        up = (ri + rb * B <= ci + col * B).astype(F32)
        zg[z, s * B:(s + 1) * B, :] = z_ref[b * B:(b + 1) * B, :] * (ok * up * zm_ref[0, b].astype(F32))
        hg[z, s * B:(s + 1) * B, :] = h_ref[b * B:(b + 1) * B, :] * (ok * hm_ref[0, b].astype(F32))

    pl.semaphore_wait(barrier, 13 + crossed.astype(jnp.int32) - homed.astype(jnp.int32))

    swap = remote(zg.at[z], sw, sw_s.at[0], sw_s.at[1], partner)

    @pl.when(crossed)
    def _():
        swap.start()

    @pl.when(jnp.logical_not(crossed))
    def _():
        sw[...] = zg[z]

    def ring(buf, ss, rs):
        made = {}

        def step(st, s):
            for d in range(2):
                if st > 0:
                    made[st - 1, s, d].wait_recv()
                if st == 3 and s % 2 != d:
                    continue
                slot = (z + 8 - st) % 8 if d == 0 else (z + st) % 8
                part = buf.at[slot, pl.ds(s * B, B)]
                cp = remote(part, part, ss.at[d, st, s], rs.at[d, st, s], zpeer[d])
                cp.start()
                made[st, s, d] = cp

        def last():
            for s in range(4):
                made[3, s, s % 2].wait_recv()

        def sent():
            for cp in made.values():
                cp.wait_send()

        return step, last, sent

    hstep, hlast, hsent = ring(hg, h_ss, h_rs)
    zstep, zlast, zsent = ring(zg, z_ss, z_rs)

    def parts(buf, hi_ref, lo_ref, dist):
        for slot in {0: [z], 4: [(z + 4) % 8]}.get(dist, [(z + dist) % 8, (z + 8 - dist) % 8]):
            hi, lo = split(buf[slot])
            hi_ref[slot] = hi
            lo_ref[slot] = lo

    for s in range(4):
        hstep(0, s)
    parts(hg, ah, al, 0)

    @pl.when(crossed)
    def _():
        swap.wait_recv()

    mine = pl.ds(pl.multiple_of(c * 256, 256), 256)
    other = pl.ds(pl.multiple_of((1 - c) * 256, 256), 256)
    cex = remote(sw.at[other], xg.at[x, mine], ce_s.at[0], ce_s.at[1], sib)
    cex.start()
    xg[x, mine, :] = sw[mine, :]
    hstep(1, 0)
    cex.wait_recv()
    xa = {}
    for d in (1, 3, 2):
        xa[d] = remote(xg.at[x], xg.at[x], xa_ss.at[d], xa_rs.at[d], xpeer[d])
        xa[d].start()
    ya = {}

    def ysend(e):
        src = (x + 4 - e) % 4
        d = (src + 4 - y) % 4
        ya[e] = d, remote(xg.at[src], z1.at[y], ya_ss.at[e], ya_rs.at[d], dev(x, src, z, c))

        @pl.when(d != 0)
        def _():
            ya[e][1].start()

    ysend(0)
    hstep(1, 1)
    hstep(1, 2)
    hstep(1, 3)
    parts(hg, ah, al, 1)
    hstep(2, 0)
    for e in (1, 3):
        xa[e].wait_recv()
        ysend(e)
    hstep(2, 1)
    hstep(2, 2)
    xa[2].wait_recv()
    ysend(2)
    z1[y] = xg[y]
    hstep(2, 3)
    parts(hg, ah, al, 2)
    for s in range(4):
        hstep(3, s)
    for s in range(4):
        zstep(0, s)
    parts(hg, ah, al, 3)
    parts(zg, bh, bl, 0)
    for d in (1, 2, 3):
        remote(xg.at[0], z1.at[y], ya_ss.at[0], ya_rs.at[d], sib).wait_recv()
    left = lax.broadcasted_iota(jnp.int32, (512, B), 1) < HALF
    for p in range(2):
        v0, v1 = z1[2 * p], z1[2 * p + 1]
        for m, v in enumerate([jnp.where(left, v0, pltpu.roll(v1, HALF, 1)),
                               jnp.where(left, pltpu.roll(v0, HALF, 1), v1)]):
            hi, lo = split(v)
            z1h[m, :, p * B:(p + 1) * B] = hi
            z1l[m, :, p * B:(p + 1) * B] = lo
    hlast()
    parts(hg, ah, al, 4)

    def whole(ref):
        return jnp.concatenate(
            [jnp.concatenate([ref[2 * q + half] for q in range(4)], axis=1) for half in range(2)], axis=0)

    crow = pl.ds(pl.multiple_of(c * 512, 512), 512)
    orow = pl.ds(pl.multiple_of((1 - c) * 512, 512), 512)

    def first(m):
        wp[m] = dot3(whole(ah), whole(al), z1h[m], z1l[m])
        cp = remote(wp.at[m, orow], cr.at[m], wc_ss.at[m], wc_rs.at[m], sib)
        cp.start()
        return cp

    def scatter(m, cp):
        cp.wait_recv()
        wc[m] = wp[m, crow, :] + cr[m]
        cps = {}
        for d in (1, 3, 2):
            piece = pl.ds(pl.multiple_of(((y + d) % 4) * B, B), B)
            cps[d] = remote(wc.at[m, piece], yr.at[m, d - 1], wy_ss.at[m, d], wy_rs.at[m, d], ypeer[d])
            cps[d].start()
        return cps

    def spread(m, cps):
        for d in (1, 3, 2):
            cps[d].wait_recv()
        r = (wc[m, pl.ds(pl.multiple_of(y * B, B), B), :] + yr[m, 0]) + (yr[m, 1] + yr[m, 2])
        wt[m, c, y] = r.T
        own = wt.at[m, c, y]
        out = {}
        for d in (1, 3, 2):
            out[d] = remote(own, own, wa_ss.at[m, d], wa_rs.at[m, d], ypeer[d])
            out[d].start()
        out[0] = remote(own, own, wf_ss.at[m, 0], wf_rs.at[m, 0], sib)
        out[0].start()
        return out

    def forward(m, out):
        fw = {}
        for d in (1, 3, 2):
            out[d].wait_recv()
            part = wt.at[m, c, (y + 4 - d) % 4]
            fw[d] = remote(part, part, wf_ss.at[m, d], wf_rs.at[m, d], sib)
            fw[d].start()
        return fw

    c0 = first(0)
    c1 = first(1)
    s0 = scatter(0, c0)
    zstep(1, 0)
    zstep(1, 1)
    s1 = scatter(1, c1)
    zstep(1, 2)
    zstep(1, 3)
    parts(zg, bh, bl, 1)
    o0 = spread(0, s0)
    for s in range(4):
        zstep(2, s)
    parts(zg, bh, bl, 2)
    o1 = spread(1, s1)
    for s in range(4):
        zstep(3, s)
    f0 = forward(0, o0)
    parts(zg, bh, bl, 3)
    zlast()
    parts(zg, bh, bl, 4)

    def second(m, out, fw):
        out[0].wait_recv()
        for d in (1, 3, 2):
            fw[d].wait_recv()
        a = jnp.concatenate([wt[m, half, s] for half in range(2) for s in range(4)], axis=1)
        hi, lo = split(a)
        t = dot3(hi, lo, whole(bh), whole(bl))
        for q in range(4):
            u[m, q] = t[q * HALF:(q + 1) * HALF, :]
        cps = {}
        for d in (1, 3, 2):
            cps[d] = remote(u.at[m, (x + d) % 4], xr.at[m, d - 1], ux_ss.at[m, d], ux_rs.at[m, d], xpeer[d])
            cps[d].start()
        return cps

    place = (zh % 2) * 2 + zl
    away = {}

    def deliver(m, cps):
        for d in (1, 3, 2):
            cps[d].wait_recv()
        v = (u[m, x] + xr[m, 0]) + (xr[m, 1] + xr[m, 2])
        for q in range(4):
            fin[m, q] = v[:, q * B:(q + 1) * B]
            to = 2 * q + zh // 2
            cp = remote(fin.at[m, q], tr.at[place, m], fd_ss.at[m, q], fd_rs.at[m, place], dev(x, y, to, c))
            away[m, q] = to, cp

            @pl.when(to == z)
            def _():
                tr[place, m] = fin[m, q]

            @pl.when(to != z)
            def _():
                cp.start()

    u0 = second(0, o0, f0)
    f1 = forward(1, o1)
    u1 = second(1, o1, f1)
    deliver(0, u0)
    deliver(1, u1)
    for m in range(CHUNKS):
        for b in range(4):
            @pl.when(zl * 4 + b != z)
            def _():
                remote(fin.at[0, 0], tr.at[b, m], fd_ss.at[0, 0], fd_rs.at[m, b], sib).wait_recv()

            out_ref[b * B + m * HALF:b * B + (m + 1) * HALF, :] = tr[b, m] * km_ref[0, b].astype(F32)

    hsent()
    zsent()

    @pl.when(crossed)
    def _():
        swap.wait_send()

    cex.wait_send()
    for d in (1, 2, 3):
        xa[d].wait_send()
    for e in range(4):
        @pl.when(ya[e][0] != 0)
        def _():
            ya[e][1].wait_send()
    for group in (s0, s1, o0, o1, f0, f1, u0, u1):
        for cp in group.values():
            cp.wait_send()
    c0.wait_send()
    c1.wait_send()
    for to, cp in away.values():
        @pl.when(to != z)
        def _():
            cp.wait_send()


def local(hamiltonian, h_mask, factor, z_mask, k_mask, block_sizes):
    dma = pltpu.SemaphoreType.DMA
    bf = jnp.bfloat16
    flags = pltpu.SMEM((1, 4), jnp.int32)
    scratch = [
        pltpu.VMEM((512, B), F32), pltpu.VMEM((512, B), F32), flags, flags, flags,
        pltpu.SMEM((32,), jnp.int32), dma((6,)),
        pltpu.VMEM((8, 512, B), F32),
        pltpu.VMEM((8, 512, B), F32),
        pltpu.VMEM((8, 512, B), bf), pltpu.VMEM((8, 512, B), bf),
        pltpu.VMEM((8, 512, B), bf), pltpu.VMEM((8, 512, B), bf),
        pltpu.VMEM((512, B), F32),
        pltpu.VMEM((4, 512, B), F32),
        pltpu.VMEM((4, 512, B), F32),
        pltpu.VMEM((CHUNKS, 512, 256), bf), pltpu.VMEM((CHUNKS, 512, 256), bf),
        pltpu.VMEM((CHUNKS, 1024, 256), F32),
        pltpu.VMEM((CHUNKS, 512, 256), F32),
        pltpu.VMEM((CHUNKS, 512, 256), F32),
        pltpu.VMEM((CHUNKS, 3, B, 256), F32),
        pltpu.VMEM((CHUNKS, 2, 4, 256, B), F32),
        pltpu.VMEM((CHUNKS, 4, HALF, 512), F32),
        pltpu.VMEM((CHUNKS, 3, HALF, 512), F32),
        pltpu.VMEM((CHUNKS, 4, HALF, B), F32),
        pltpu.VMEM((4, CHUNKS, HALF, B), F32),
        dma((2, 4, 4)), dma((2, 4, 4)), dma((2, 4, 4)), dma((2, 4, 4)),
        dma((2,)), dma((2,)), dma((4,)), dma((4,)), dma((4,)), dma((4,)),
        dma((2,)), dma((2,)), dma((2, 4)), dma((2, 4)), dma((2, 4)), dma((2, 4)),
        dma((2, 4)), dma((2, 4)), dma((2, 4)), dma((2, 4)), dma((2, 4)), dma((2, 4)),
    ]
    hbm = pl.BlockSpec(memory_space=pltpu.HBM)
    return pl.pallas_call(
        kernel,
        out_shape=jax.ShapeDtypeStruct((512, B), F32),
        in_specs=[hbm] * 6,
        out_specs=pl.BlockSpec(memory_space=pltpu.VMEM),
        scratch_shapes=scratch,
        compiler_params=pltpu.CompilerParams(
            collective_id=0, has_side_effects=True, vmem_limit_bytes=64 << 20),
        name="congruence",
    )(hamiltonian, h_mask.reshape(1, 4), factor, z_mask.reshape(1, 4), k_mask.reshape(1, 4), block_sizes)


def solution(mesh):
    placed = (
        P("row", "col"),
        P("row", "col"),
        P("row", "col"),
        P("row", "col"),
        P("row", "col"),
        P(),
    )
    return jax.shard_map(
        local, mesh=mesh, in_specs=placed, out_specs=P("row", "col"), check_vma=False
    )
```

time: 119 us -> 91.5 us (0.77)
  the two profiles are of different devices: /device:TPU:34 before, /device:TPU:48 now
where the time goes in v2:
time: 91.5 us; the launch traced here: 91.4 us
  Pallas kernels  89.7 us (98%)
  local copies, waits for them, and re-layouts  1.67 us (2%)
    pallas_call x1, Pallas kernels, local(): pl.pallas_call(kernel, out_shape=jax.ShapeDtypeStruct((512, B), F32), in_...  89.7 us

profile of v2, /device:TPU:48, one launch (start us, length us, event | category | flops | bytes accessed | tf_op | source)
XLA Modules:
  0.0 91.4 jit_solution(6666730688554398756)
XLA Ops:
  0.0 89.7 %congruence.1 = f32[512,128]{1,0:T(8,128)} custom-call(f32[512,128]{1,0:T(8,128)} %h_hbm.1, s32[1,4]{1,0:T(1,128)} %bitcast.3, f32[512,128]{1,0:T(8,128)} %z_hbm.1, s32[1,4]{1,0:T(1,128)} %bitcast.4, s32[1,4]{1,0:T(1,128)} %bitcast.5, s32[32]{0:T(128)} %size_hbm.1), custom_call_target="tpu_custom_call" | custom-call | tf_op jit(solution)/shard_map/congruence/pallas_call | solution.py:367
  89.7 1.7 %copy.8 = f32[512,128]{1,0:T(8,128)} copy(f32[512,128]{1,0:T(8,128)} %congruence.1) | data formatting | bytes 524288

commit v3 on v2

v3 whole, which is shorter than its diff:
```python
import jax
import jax.numpy as jnp
from jax import lax
from jax.experimental import pallas as pl
from jax.experimental.pallas import tpu as pltpu
from jax.sharding import PartitionSpec as P

B = 128
MESH = pl.DeviceIdType.MESH
ORDER = (0, 2, 1, 3)
F32 = jnp.float32
CHUNKS = 2
HALF = B // CHUNKS


def split(v):
    hi = v.astype(jnp.bfloat16)
    return hi, (v - hi.astype(F32)).astype(jnp.bfloat16)


def dot3(ah, al, bh, bl, axis):
    return lax.dot_general(
        jnp.concatenate([ah, ah, al], axis=1), jnp.concatenate([bh, bl, bh], axis=axis),
        (((1,), (axis,)), ((), ())), preferred_element_type=F32)


def kernel(h_hbm, hm_hbm, z_hbm, zm_hbm, km_hbm, size_hbm, out_ref,
           h_ref, z_ref, hm_ref, zm_ref, km_ref, size_ref, in_s,
           hg, zg, ah, al, bh, bl, sw, z1, z1h, z1l, wp, cr, wc, yr, wt, u, xr, fin, tr,
           h_ss, h_rs, z_ss, z_rs, sw_s, z1_ss, z1_rs,
           wc_ss, wc_rs, wy_ss, wy_rs, wa_ss, wa_rs, wf_ss, wf_rs, ux_ss, ux_rs, fd_ss, fd_rs):
    row = lax.axis_index("row")
    col = lax.axis_index("col")
    x, zl = row // 2, row % 2
    y, zh, c = col // 8, (col // 2) % 4, col % 2
    z = zh * 2 + zl

    loads = [
        pltpu.make_async_copy(src, dst, in_s.at[i])
        for i, (src, dst) in enumerate([
            (size_hbm, size_ref), (zm_hbm, zm_ref), (z_hbm, z_ref), (hm_hbm, hm_ref), (h_hbm, h_ref), (km_hbm, km_ref)])
    ]
    for cp in loads:
        cp.start()

    def dev(x_, y_, z_, c_):
        return (x_ * 2 + z_ % 2, (y_ * 4 + z_ // 2) * 2 + c_)

    def remote(src, dst, ss, rs, to):
        return pltpu.make_async_remote_copy(
            src_ref=src, dst_ref=dst, send_sem=ss, recv_sem=rs, device_id=to, device_id_type=MESH)

    sib = dev(x, y, z, 1 - c)
    xpeer = [None] + [dev((x + d) % 4, y, z, c) for d in (1, 2, 3)]
    ypeer = [None] + [dev(x, (y + d) % 4, z, c) for d in (1, 2, 3)]
    zpeer = [dev(x, y, (z + 1) % 8, c), dev(x, y, (z + 7) % 8, c)]
    partner = dev(x, y, zh * 2 + c, zl)
    crossed = zl != c
    homed = zl == zh // 2
    diag = x == y

    barrier = pltpu.get_barrier_semaphore()
    for to in [sib] + xpeer[1:] + ypeer[1:] + zpeer:
        pl.semaphore_signal(barrier, inc=1, device_id=to, device_id_type=MESH)

    @pl.when(crossed)
    def _():
        pl.semaphore_signal(barrier, inc=1, device_id=partner, device_id_type=MESH)

    for b in range(4):
        @pl.when(zl * 4 + b != z)
        def _():
            pl.semaphore_signal(barrier, inc=1, device_id=dev(x, y, zl * 4 + b, c), device_id_type=MESH)

    for q in range(4):
        for p in range(2):
            @pl.when(jnp.logical_not(jnp.logical_and(diag, jnp.logical_and(y == q, c == p))))
            def _():
                pl.semaphore_signal(barrier, inc=1, device_id=dev(y, q, z, p), device_id_type=MESH)

    for cp in loads:
        cp.wait()
    ri = lax.broadcasted_iota(jnp.int32, (B, B), 0)
    ci = lax.broadcasted_iota(jnp.int32, (B, B), 1)
    colok = ci < size_ref[col]
    for s, b in enumerate(ORDER):
        rb = row * 4 + b
        ok = jnp.logical_and(colok, ri < size_ref[rb]).astype(F32)
        up = (ri + rb * B <= ci + col * B).astype(F32)
        zg[z, s * B:(s + 1) * B, :] = z_ref[b * B:(b + 1) * B, :] * (ok * up * zm_ref[0, b].astype(F32))
        hg[z, s * B:(s + 1) * B, :] = h_ref[b * B:(b + 1) * B, :] * (ok * hm_ref[0, b].astype(F32))

    pl.semaphore_wait(barrier, 21 + crossed.astype(jnp.int32) - homed.astype(jnp.int32) - diag.astype(jnp.int32))

    swap = remote(zg.at[z], sw, sw_s.at[0], sw_s.at[1], partner)

    @pl.when(crossed)
    def _():
        swap.start()

    @pl.when(jnp.logical_not(crossed))
    def _():
        sw[...] = zg[z]

    def ring(buf, ss, rs):
        made = {}

        def step(st, s):
            for d in range(2):
                if st > 0:
                    made[st - 1, s, d].wait_recv()
                if st == 3 and s % 2 != d:
                    continue
                slot = (z + 8 - st) % 8 if d == 0 else (z + st) % 8
                part = buf.at[slot, pl.ds(s * B, B)]
                cp = remote(part, part, ss.at[d, st, s], rs.at[d, st, s], zpeer[d])
                cp.start()
                made[st, s, d] = cp

        def last():
            for s in range(4):
                made[3, s, s % 2].wait_recv()

        def sent():
            for cp in made.values():
                cp.wait_send()

        return step, last, sent

    hstep, hlast, hsent = ring(hg, h_ss, h_rs)
    zstep, zlast, zsent = ring(zg, z_ss, z_rs)

    def parts(buf, hi_ref, lo_ref, dist):
        for slot in {0: [z], 4: [(z + 4) % 8]}.get(dist, [(z + dist) % 8, (z + 8 - dist) % 8]):
            hi, lo = split(buf[slot])
            hi_ref[slot] = hi
            lo_ref[slot] = lo

    for s in range(4):
        hstep(0, s)
    parts(hg, ah, al, 0)

    @pl.when(crossed)
    def _():
        swap.wait_recv()

    zrow = pl.ds(pl.multiple_of(c * 256, 256), 256)
    sends = []
    for d in (2, 1, 3, 0):
        for p in range(2):
            cp = remote(sw.at[pl.ds(p * 256, 256)], z1.at[y, zrow], z1_ss.at[d, p], z1_rs.at[y, c],
                        dev((x + d) % 4, x, z, p))
            own = jnp.logical_and(diag, c == p) if d == 0 else None
            sends.append((own, cp))
            if own is None:
                cp.start()
            else:
                pl.when(jnp.logical_not(own))(cp.start)

                @pl.when(own)
                def _():
                    z1[y, zrow, :] = sw[p * 256:(p + 1) * 256, :]

    for st in (1, 2, 3):
        for s in range(4):
            hstep(st, s)
        parts(hg, ah, al, st)
    for s in range(4):
        zstep(0, s)
    parts(zg, bh, bl, 0)
    for q in range(4):
        for p in range(2):
            @pl.when(jnp.logical_not(jnp.logical_and(diag, jnp.logical_and(y == q, c == p))))
            def _():
                remote(sw.at[pl.ds(0, 256)], z1.at[q, pl.ds(p * 256, 256)], z1_ss.at[0, 0], z1_rs.at[q, p], sib).wait_recv()

        hi, lo = split(z1[q].T)
        for m in range(CHUNKS):
            z1h[m, q * HALF:(q + 1) * HALF, :] = hi[m * HALF:(m + 1) * HALF, :]
            z1l[m, q * HALF:(q + 1) * HALF, :] = lo[m * HALF:(m + 1) * HALF, :]

    def whole(ref):
        return jnp.concatenate(
            [jnp.concatenate([ref[2 * q + half] for q in range(4)], axis=1) for half in range(2)], axis=0)

    kz = [1 - zl, zl]
    myrow = pl.ds(pl.multiple_of(y * HALF, HALF), HALF)

    def first(k, m):
        rh, rl = [jnp.concatenate([ref[2 * q + kz[k]] for q in range(4)], axis=1) for ref in (ah, al)]
        t = dot3(z1h[m], z1l[m], rh, rl, 1)
        wp[k, m, 0] = t[:, :256]
        wp[k, m, 1] = t[:, 256:]
        cp = remote(wp.at[k, m, 1 - c], cr.at[k, m], wc_ss.at[k, m], wc_rs.at[k, m], sib)
        cp.start()
        return cp

    def scatter(k, m, cp):
        cp.wait_recv()
        wc[k, m] = wp[k, m, c] + cr[k, m]
        cps = {}
        for d in (2, 1, 3):
            piece = pl.ds(pl.multiple_of(((y + d) % 4) * HALF, HALF), HALF)
            cps[d] = remote(wc.at[k, m, piece], yr.at[k, m, d - 1], wy_ss.at[k, m, d], wy_rs.at[k, m, d], ypeer[d])
            cps[d].start()
        return cps

    def spread(k, m, cps):
        for d in (1, 3, 2):
            cps[d].wait_recv()
        wt[m, kz[k], c, myrow, :] = (wc[k, m, myrow, :] + yr[k, m, 0]) + (yr[k, m, 1] + yr[k, m, 2])
        own = wt.at[m, kz[k], c, myrow]
        out = {}
        for d in (2, 1, 3):
            out[d] = remote(own, own, wa_ss.at[k, m, d], wa_rs.at[k, m, d], ypeer[d])
            out[d].start()
        out[0] = remote(own, own, wf_ss.at[k, m, 0], wf_rs.at[k, m, 0], sib)
        out[0].start()
        return out

    def forward(k, m, out):
        for d in (1, 3, 2):
            out[d].wait_recv()
            part = wt.at[m, kz[k], c, pl.ds(pl.multiple_of(((y + 4 - d) % 4) * HALF, HALF), HALF)]
            out[d + 3] = remote(part, part, wf_ss.at[k, m, d], wf_rs.at[k, m, d], sib)
            out[d + 3].start()

    c00 = first(0, 0)
    c01 = first(0, 1)
    hlast()
    parts(hg, ah, al, 4)
    s00 = scatter(0, 0, c00)
    c10 = first(1, 0)
    s01 = scatter(0, 1, c01)
    c11 = first(1, 1)
    s10 = scatter(1, 0, c10)
    o00 = spread(0, 0, s00)
    s11 = scatter(1, 1, c11)
    zstep(1, 0)
    zstep(1, 1)
    o01 = spread(0, 1, s01)
    zstep(1, 2)
    zstep(1, 3)
    parts(zg, bh, bl, 1)
    forward(0, 0, o00)
    o10 = spread(1, 0, s10)
    zstep(2, 0)
    zstep(2, 1)
    o11 = spread(1, 1, s11)
    forward(0, 1, o01)
    zstep(2, 2)
    zstep(2, 3)
    parts(zg, bh, bl, 2)
    zstep(3, 0)
    zstep(3, 1)
    forward(1, 0, o10)
    zstep(3, 2)
    zstep(3, 3)
    parts(zg, bh, bl, 3)
    zlast()
    parts(zg, bh, bl, 4)

    def second(m, outs):
        for out in outs:
            for d in (0, 4, 5, 6):
                out[d].wait_recv()
        hi, lo = split(jnp.concatenate([wt[m, half, p] for half in range(2) for p in range(2)], axis=1))
        t = dot3(hi, lo, whole(bh), whole(bl), 0)
        for q in range(4):
            u[m, q] = t[q * HALF:(q + 1) * HALF, :]
        cps = {}
        for d in (1, 3, 2):
            cps[d] = remote(u.at[m, (x + d) % 4], xr.at[m, d - 1], ux_ss.at[m, d], ux_rs.at[m, d], xpeer[d])
            cps[d].start()
        return cps

    place = (zh % 2) * 2 + zl
    away = {}

    def deliver(m, cps):
        for d in (1, 3, 2):
            cps[d].wait_recv()
        v = (u[m, x] + xr[m, 0]) + (xr[m, 1] + xr[m, 2])
        for q in range(4):
            fin[m, q] = v[:, q * B:(q + 1) * B]
            to = 2 * q + zh // 2
            cp = remote(fin.at[m, q], tr.at[place, m], fd_ss.at[m, q], fd_rs.at[m, place], dev(x, y, to, c))
            away[m, q] = to, cp

            @pl.when(to == z)
            def _():
                tr[place, m] = fin[m, q]

            @pl.when(to != z)
            def _():
                cp.start()

    u0 = second(0, (o00, o10))
    forward(1, 1, o11)
    u1 = second(1, (o01, o11))
    deliver(0, u0)
    deliver(1, u1)
    for m in range(CHUNKS):
        for b in range(4):
            @pl.when(zl * 4 + b != z)
            def _():
                remote(fin.at[0, 0], tr.at[b, m], fd_ss.at[0, 0], fd_rs.at[m, b], sib).wait_recv()

            out_ref[b * B + m * HALF:b * B + (m + 1) * HALF, :] = tr[b, m] * km_ref[0, b].astype(F32)

    hsent()
    zsent()

    @pl.when(crossed)
    def _():
        swap.wait_send()

    for own, cp in sends:
        if own is None:
            cp.wait_send()
        else:
            pl.when(jnp.logical_not(own))(cp.wait_send)
    for group in (s00, s01, s10, s11, o00, o01, o10, o11, u0, u1):
        for cp in group.values():
            cp.wait_send()
    for cp in (c00, c01, c10, c11):
        cp.wait_send()
    for to, cp in away.values():
        @pl.when(to != z)
        def _():
            cp.wait_send()


def local(hamiltonian, h_mask, factor, z_mask, k_mask, block_sizes):
    dma = pltpu.SemaphoreType.DMA
    bf = jnp.bfloat16
    flags = pltpu.SMEM((1, 4), jnp.int32)
    scratch = [
        pltpu.VMEM((512, B), F32), pltpu.VMEM((512, B), F32), flags, flags, flags,
        pltpu.SMEM((32,), jnp.int32), dma((6,)),
        pltpu.VMEM((8, 512, B), F32),
        pltpu.VMEM((8, 512, B), F32),
        pltpu.VMEM((8, 512, B), bf), pltpu.VMEM((8, 512, B), bf),
        pltpu.VMEM((8, 512, B), bf), pltpu.VMEM((8, 512, B), bf),
        pltpu.VMEM((512, B), F32),
        pltpu.VMEM((4, 512, B), F32),
        pltpu.VMEM((CHUNKS, 256, 512), bf), pltpu.VMEM((CHUNKS, 256, 512), bf),
        pltpu.VMEM((2, CHUNKS, 2, 256, 256), F32),
        pltpu.VMEM((2, CHUNKS, 256, 256), F32),
        pltpu.VMEM((2, CHUNKS, 256, 256), F32),
        pltpu.VMEM((2, CHUNKS, 3, HALF, 256), F32),
        pltpu.VMEM((CHUNKS, 2, 2, 256, 256), F32),
        pltpu.VMEM((CHUNKS, 4, HALF, 512), F32),
        pltpu.VMEM((CHUNKS, 3, HALF, 512), F32),
        pltpu.VMEM((CHUNKS, 4, HALF, B), F32),
        pltpu.VMEM((4, CHUNKS, HALF, B), F32),
        dma((2, 4, 4)), dma((2, 4, 4)), dma((2, 4, 4)), dma((2, 4, 4)),
        dma((2,)), dma((4, 2)), dma((4, 2)),
        dma((2, 2)), dma((2, 2)), dma((2, 2, 4)), dma((2, 2, 4)), dma((2, 2, 4)), dma((2, 2, 4)),
        dma((2, 2, 4)), dma((2, 2, 4)), dma((2, 4)), dma((2, 4)), dma((2, 4)), dma((2, 4)),
    ]
    hbm = pl.BlockSpec(memory_space=pltpu.HBM)
    return pl.pallas_call(
        kernel,
        out_shape=jax.ShapeDtypeStruct((512, B), F32),
        in_specs=[hbm] * 6,
        out_specs=pl.BlockSpec(memory_space=pltpu.VMEM),
        scratch_shapes=scratch,
        compiler_params=pltpu.CompilerParams(
            collective_id=0, has_side_effects=True, vmem_limit_bytes=48 << 20),
        name="congruence",
    )(*[pltpu.with_memory_space_constraint(v, pltpu.HBM) for v in (
        hamiltonian, h_mask.reshape(1, 4), factor, z_mask.reshape(1, 4), k_mask.reshape(1, 4), block_sizes)])


def solution(mesh):
    placed = (
        P("row", "col"),
        P("row", "col"),
        P("row", "col"),
        P("row", "col"),
        P("row", "col"),
        P(),
    )
    return jax.shard_map(
        local, mesh=mesh, in_specs=placed, out_specs=P("row", "col"), check_vma=False
    )
```

time: 91.5 us -> 85.9 us (0.939)
  the two profiles are of different devices: /device:TPU:48 before, /device:TPU:34 now
where the time goes in v3:
time: 85.9 us; the launch traced here: 84.2 us
  Pallas kernels  83.5 us (97%)
    pallas_call x1, Pallas kernels, local(): pl.pallas_call(kernel, out_shape=jax.ShapeDtypeStruct((512, B), F32), in_...  83.5 us

profile of v3, /device:TPU:34, one launch (start us, length us, event | category | flops | bytes accessed | tf_op | source)
XLA Modules:
  0.0 84.2 jit_solution(216210115857257295)
XLA Ops:
  0.0 83.5 %congruence.1 = f32[512,128]{1,0:T(8,128)S(1)} custom-call(f32[512,128]{1,0:T(8,128)} %h_hbm.1, s32[1,4]{1,0:T(1,128)} %bitcast.3, f32[512,128]{1,0:T(8,128)} %z_hbm.1, s32[1,4]{1,0:T(1,128)} %bitcast.4, s32[1,4]{1,0:T(1,128)} %bitcast.5, s32[32]{0:T(128)} %size_hbm.1), custom_call_target="tpu_custom_call" | custom-call | tf_op jit(solution)/shard_map/congruence/pallas_call | solution.py:363
  83.5 0.7 copy.8

commit v4 on v3

--- a/solution.py
+++ b/solution.py
@@ -18,6 +18,13 @@
     return hi, (v - hi.astype(F32)).astype(jnp.bfloat16)
 
 
+def when(cond, act):
+    if cond is None:
+        act()
+    else:
+        pl.when(cond)(act)
+
+
 def dot3(ah, al, bh, bl, axis):
     return lax.dot_general(
         jnp.concatenate([ah, ah, al], axis=1), jnp.concatenate([bh, bl, bh], axis=axis),
@@ -26,9 +33,9 @@
 
 def kernel(h_hbm, hm_hbm, z_hbm, zm_hbm, km_hbm, size_hbm, out_ref,
            h_ref, z_ref, hm_ref, zm_ref, km_ref, size_ref, in_s,
-           hg, zg, ah, al, bh, bl, sw, z1, z1h, z1l, wp, cr, wc, yr, wt, u, xr, fin, tr,
+           hg, zg, ah, al, bh, bl, sw, z1, z1h, z1l, wp, cr, wc, yr, wt, wh, wl, u, xr, fin, fint, tr,
            h_ss, h_rs, z_ss, z_rs, sw_s, z1_ss, z1_rs,
-           wc_ss, wc_rs, wy_ss, wy_rs, wa_ss, wa_rs, wf_ss, wf_rs, ux_ss, ux_rs, fd_ss, fd_rs):
+           wc_ss, wc_rs, wy_ss, wy_rs, wa_ss, wa_rs, wf_ss, wf_rs, ux_ss, ux_rs, fd_ss, fm_ss, fd_rs):
     row = lax.axis_index("row")
     col = lax.axis_index("col")
     x, zl = row // 2, row % 2
@@ -67,8 +74,14 @@
     def _():
         pl.semaphore_signal(barrier, inc=1, device_id=partner, device_id_type=MESH)
 
+    lower = x >= y
+    for p in range(2):
+        @pl.when(x < y)
+        def _():
+            pl.semaphore_signal(barrier, inc=1, device_id=dev(y, x, 2 * zh + c, p), device_id_type=MESH)
+
     for b in range(4):
-        @pl.when(zl * 4 + b != z)
+        @pl.when(jnp.logical_and(lower, zl * 4 + b != z))
         def _():
             pl.semaphore_signal(barrier, inc=1, device_id=dev(x, y, zl * 4 + b, c), device_id_type=MESH)
 
@@ -90,7 +103,8 @@
         zg[z, s * B:(s + 1) * B, :] = z_ref[b * B:(b + 1) * B, :] * (ok * up * zm_ref[0, b].astype(F32))
         hg[z, s * B:(s + 1) * B, :] = h_ref[b * B:(b + 1) * B, :] * (ok * hm_ref[0, b].astype(F32))
 
-    pl.semaphore_wait(barrier, 21 + crossed.astype(jnp.int32) - homed.astype(jnp.int32) - diag.astype(jnp.int32))
+    greets = jnp.where(lower, 4 - homed.astype(jnp.int32), 0) + jnp.where(x > y, 2, 0)
+    pl.semaphore_wait(barrier, 17 + crossed.astype(jnp.int32) - diag.astype(jnp.int32) + greets)
 
     swap = remote(zg.at[z], sw, sw_s.at[0], sw_s.at[1], partner)
 
@@ -117,8 +131,8 @@
                 cp.start()
                 made[st, s, d] = cp
 
-        def last():
-            for s in range(4):
+        def last(subs):
+            for s in subs:
                 made[3, s, s % 2].wait_recv()
 
         def sent():
@@ -130,13 +144,14 @@
     hstep, hlast, hsent = ring(hg, h_ss, h_rs)
     zstep, zlast, zsent = ring(zg, z_ss, z_rs)
 
-    def parts(buf, hi_ref, lo_ref, dist):
+    def parts(buf, hi_ref, lo_ref, dist, rows=slice(0, 512)):
         for slot in {0: [z], 4: [(z + 4) % 8]}.get(dist, [(z + dist) % 8, (z + 8 - dist) % 8]):
-            hi, lo = split(buf[slot])
-            hi_ref[slot] = hi
-            lo_ref[slot] = lo
-
-    for s in range(4):
+            hi, lo = split(buf[slot, rows, :])
+            hi_ref[slot, rows, :] = hi
+            lo_ref[slot, rows, :] = lo
+
+    pair = (slice(0, 256), slice(256, 512))
+    for s in (0, 1, 2):
         hstep(0, s)
     parts(hg, ah, al, 0)
 
@@ -161,13 +176,20 @@
                 def _():
                     z1[y, zrow, :] = sw[p * 256:(p + 1) * 256, :]
 
-    for st in (1, 2, 3):
-        for s in range(4):
-            hstep(st, s)
-        parts(hg, ah, al, st)
-    for s in range(4):
-        zstep(0, s)
-    parts(zg, bh, bl, 0)
+    hstep(1, 0)
+    hstep(1, 1)
+    parts(hg, ah, al, 1, pair[0])
+    hstep(0, 3)
+    hstep(2, 0)
+    hstep(2, 1)
+    parts(hg, ah, al, 2, pair[0])
+    hstep(1, 2)
+    hstep(3, 0)
+    hstep(3, 1)
+    parts(hg, ah, al, 3, pair[0])
+    hstep(1, 3)
+    parts(hg, ah, al, 1, pair[1])
+    hstep(2, 2)
     for q in range(4):
         for p in range(2):
             @pl.when(jnp.logical_not(jnp.logical_and(diag, jnp.logical_and(y == q, c == p))))
@@ -179,15 +201,15 @@
             z1h[m, q * HALF:(q + 1) * HALF, :] = hi[m * HALF:(m + 1) * HALF, :]
             z1l[m, q * HALF:(q + 1) * HALF, :] = lo[m * HALF:(m + 1) * HALF, :]
 
-    def whole(ref):
-        return jnp.concatenate(
-            [jnp.concatenate([ref[2 * q + half] for q in range(4)], axis=1) for half in range(2)], axis=0)
-
-    kz = [1 - zl, zl]
+    hlast((0, 1))
+    parts(hg, ah, al, 4, pair[0])
     myrow = pl.ds(pl.multiple_of(y * HALF, HALF), HALF)
 
     def first(k, m):
-        rh, rl = [jnp.concatenate([ref[2 * q + kz[k]] for q in range(4)], axis=1) for ref in (ah, al)]
+        rh, rl = [
+            jnp.concatenate(
+                [jnp.concatenate([ref[2 * q + half, pair[k], :] for q in range(4)], axis=1) for half in range(2)], axis=0)
+            for ref in (ah, al)]
         t = dot3(z1h[m], z1l[m], rh, rl, 1)
         wp[k, m, 0] = t[:, :256]
         wp[k, m, 1] = t[:, 256:]
@@ -201,112 +223,167 @@
         cps = {}
         for d in (2, 1, 3):
             piece = pl.ds(pl.multiple_of(((y + d) % 4) * HALF, HALF), HALF)
-            cps[d] = remote(wc.at[k, m, piece], yr.at[k, m, d - 1], wy_ss.at[k, m, d], wy_rs.at[k, m, d], ypeer[d])
-            cps[d].start()
+            cond = jnp.logical_and(y + d < 4, y + d >= x)
+            cps[d] = cond, remote(
+                wc.at[k, m, piece], yr.at[k, m, d - 1], wy_ss.at[k, m, d], wy_rs.at[k, m, d], ypeer[d])
+            when(cond, cps[d][1].start)
         return cps
 
     def spread(k, m, cps):
+        wt[m, k, c, myrow, :] = wc[k, m, myrow, :]
         for d in (1, 3, 2):
-            cps[d].wait_recv()
-        wt[m, kz[k], c, myrow, :] = (wc[k, m, myrow, :] + yr[k, m, 0]) + (yr[k, m, 1] + yr[k, m, 2])
-        own = wt.at[m, kz[k], c, myrow]
+            @pl.when(jnp.logical_and(d <= y, x <= y))
+            def _():
+                cps[d][1].wait_recv()
+                wt[m, k, c, myrow, :] += yr[k, m, d - 1]
+
+        own = wt.at[m, k, c, myrow]
         out = {}
         for d in (2, 1, 3):
-            out[d] = remote(own, own, wa_ss.at[k, m, d], wa_rs.at[k, m, d], ypeer[d])
-            out[d].start()
-        out[0] = remote(own, own, wf_ss.at[k, m, 0], wf_rs.at[k, m, 0], sib)
-        out[0].start()
+            cond = jnp.logical_and(y + d >= 4, y + d - 4 >= x)
+            out[d] = cond, remote(own, own, wa_ss.at[k, m, d], wa_rs.at[k, m, d], ypeer[d])
+            when(cond, out[d][1].start)
+        out[0] = None, remote(own, own, wf_ss.at[k, m, 0], wf_rs.at[k, m, 0], sib)
+        out[0][1].start()
         return out
 
     def forward(k, m, out):
         for d in (1, 3, 2):
-            out[d].wait_recv()
-            part = wt.at[m, kz[k], c, pl.ds(pl.multiple_of(((y + 4 - d) % 4) * HALF, HALF), HALF)]
-            out[d + 3] = remote(part, part, wf_ss.at[k, m, d], wf_rs.at[k, m, d], sib)
-            out[d + 3].start()
+            part = wt.at[m, k, c, pl.ds(pl.multiple_of(((y + 4 - d) % 4) * HALF, HALF), HALF)]
+            cond = jnp.logical_and(d > y, x <= y)
+            out[d + 3] = cond, remote(part, part, wf_ss.at[k, m, d], wf_rs.at[k, m, d], sib)
+
+            @pl.when(cond)
+            def _():
+                out[d][1].wait_recv()
+                out[d + 3][1].start()
+
+    def gathered(k, m, out):
+        for d in (0, 4, 5, 6):
+            when(out[d][0], out[d][1].wait_recv)
+        for half in range(2):
+            hi, lo = split(wt[m, k, half])
+            at = (k * 2 + half) * 256
+            for q in range(4):
+                wh[q * B + m * HALF:q * B + (m + 1) * HALF, at:at + 256] = hi[q * HALF:(q + 1) * HALF, :]
+                wl[q * B + m * HALF:q * B + (m + 1) * HALF, at:at + 256] = lo[q * HALF:(q + 1) * HALF, :]
 
     c00 = first(0, 0)
+    hstep(2, 3)
     c01 = first(0, 1)
-    hlast()
-    parts(hg, ah, al, 4)
+    zstep(0, 0)
+    hstep(3, 2)
     s00 = scatter(0, 0, c00)
+    zstep(0, 1)
+    parts(hg, ah, al, 2, pair[1])
+    s01 = scatter(0, 1, c01)
+    hstep(3, 3)
+    zstep(0, 2)
+    zstep(0, 3)
+    parts(hg, ah, al, 3, pair[1])
+    parts(zg, bh, bl, 0)
+    hlast((2, 3))
+    parts(hg, ah, al, 4, pair[1])
     c10 = first(1, 0)
-    s01 = scatter(0, 1, c01)
+    o00 = spread(0, 0, s00)
+    zstep(1, 0)
     c11 = first(1, 1)
+    zstep(1, 1)
     s10 = scatter(1, 0, c10)
-    o00 = spread(0, 0, s00)
-    s11 = scatter(1, 1, c11)
-    zstep(1, 0)
-    zstep(1, 1)
     o01 = spread(0, 1, s01)
     zstep(1, 2)
+    s11 = scatter(1, 1, c11)
     zstep(1, 3)
     parts(zg, bh, bl, 1)
     forward(0, 0, o00)
-    o10 = spread(1, 0, s10)
     zstep(2, 0)
     zstep(2, 1)
-    o11 = spread(1, 1, s11)
-    forward(0, 1, o01)
+    o10 = spread(1, 0, s10)
+    gathered(0, 0, o00)
     zstep(2, 2)
     zstep(2, 3)
     parts(zg, bh, bl, 2)
+    forward(0, 1, o01)
     zstep(3, 0)
+    gathered(0, 1, o01)
     zstep(3, 1)
-    forward(1, 0, o10)
+    o11 = spread(1, 1, s11)
     zstep(3, 2)
     zstep(3, 3)
     parts(zg, bh, bl, 3)
-    zlast()
-    parts(zg, bh, bl, 4)
-
-    def second(m, outs):
-        for out in outs:
-            for d in (0, 4, 5, 6):
-                out[d].wait_recv()
-        hi, lo = split(jnp.concatenate([wt[m, half, p] for half in range(2) for p in range(2)], axis=1))
-        t = dot3(hi, lo, whole(bh), whole(bl), 0)
-        for q in range(4):
-            u[m, q] = t[q * HALF:(q + 1) * HALF, :]
-        cps = {}
-        for d in (1, 3, 2):
-            cps[d] = remote(u.at[m, (x + d) % 4], xr.at[m, d - 1], ux_ss.at[m, d], ux_rs.at[m, d], xpeer[d])
-            cps[d].start()
-        return cps
+    forward(1, 0, o10)
+    gathered(1, 0, o10)
+    forward(1, 1, o11)
+    gathered(1, 1, o11)
+
+    shift = zl * 2 + 3
+    near = [zh, (zh + shift) % 4, (zh + 4 - shift % 4) % 4, (zh + 2) % 4]
+
+    def second(js):
+        rh, rl = [
+            jnp.concatenate(
+                [jnp.concatenate([ref[2 * near[j] + half, pair[k], :] for k in range(2) for half in range(2)], axis=0)
+                 for j in js], axis=1)
+            for ref in (bh, bl)]
+        t = dot3(wh[...], wl[...], rh, rl, 0)
+        outs = []
+        for i, j in enumerate(js):
+            for q in range(4):
+                u[j, q] = t[q * B:(q + 1) * B, i * B:(i + 1) * B]
+            cps = {}
+            for d in (2, 1, 3):
+                q = (x + d) % 4
+                cond = jnp.logical_and(x <= y, q >= y)
+                cps[d] = cond, remote(u.at[j, q], xr.at[j, d - 1], ux_ss.at[j, d], ux_rs.at[j, d], xpeer[d])
+                when(cond, cps[d][1].start)
+            outs.append(cps)
+        return outs
 
     place = (zh % 2) * 2 + zl
     away = {}
 
-    def deliver(m, cps):
+    def deliver(j, cps):
+        fin[j] = jnp.where(diag, u[j, x], 0.0)
         for d in (1, 3, 2):
-            cps[d].wait_recv()
-        v = (u[m, x] + xr[m, 0]) + (xr[m, 1] + xr[m, 2])
-        for q in range(4):
-            fin[m, q] = v[:, q * B:(q + 1) * B]
-            to = 2 * q + zh // 2
-            cp = remote(fin.at[m, q], tr.at[place, m], fd_ss.at[m, q], fd_rs.at[m, place], dev(x, y, to, c))
-            away[m, q] = to, cp
-
-            @pl.when(to == z)
+            @pl.when(jnp.logical_and(lower, (x + 4 - d) % 4 <= y))
             def _():
-                tr[place, m] = fin[m, q]
-
-            @pl.when(to != z)
-            def _():
-                cp.start()
-
-    u0 = second(0, (o00, o10))
-    forward(1, 1, o11)
-    u1 = second(1, (o01, o11))
+                cps[d][1].wait_recv()
+                fin[j] += xr[j, d - 1]
+
+        to = 2 * near[j] + zh // 2
+        slot = (near[j] % 2) * 2 + c
+        away[j] = [
+            (jnp.logical_and(lower, to != z),
+             remote(fin.at[j], tr.at[place], fd_ss.at[j], fd_rs.at[place], dev(x, y, to, c))),
+            (x > y,
+             remote(fint.at[j], tr.at[slot], fm_ss.at[j], fd_rs.at[slot], dev(y, x, 2 * zh + near[j] // 2, zl))),
+        ]
+        when(away[j][0][0], away[j][0][1].start)
+
+        @pl.when(x > y)
+        def _():
+            fint[j] = fin[j].T
+            away[j][1][1].start()
+
+        @pl.when(jnp.logical_and(lower, to == z))
+        def _():
+            tr[place] = fin[j]
+
+    u0, u1 = second((0, 1))
+    (u2,) = second((2,))
     deliver(0, u0)
     deliver(1, u1)
-    for m in range(CHUNKS):
-        for b in range(4):
-            @pl.when(zl * 4 + b != z)
-            def _():
-                remote(fin.at[0, 0], tr.at[b, m], fd_ss.at[0, 0], fd_rs.at[m, b], sib).wait_recv()
-
-            out_ref[b * B + m * HALF:b * B + (m + 1) * HALF, :] = tr[b, m] * km_ref[0, b].astype(F32)
+    zlast(range(4))
+    parts(zg, bh, bl, 4)
+    (u3,) = second((3,))
+    deliver(2, u2)
+    deliver(3, u3)
+    for b in range(4):
+        @pl.when(jnp.logical_not(jnp.logical_and(lower, zl * 4 + b == z)))
+        def _():
+            remote(fin.at[0], tr.at[b], fd_ss.at[0], fd_rs.at[b], sib).wait_recv()
+
+        out_ref[b * B:(b + 1) * B, :] = tr[b] * km_ref[0, b].astype(F32)
 
     hsent()
     zsent()
@@ -320,15 +397,14 @@
             cp.wait_send()
         else:
             pl.when(jnp.logical_not(own))(cp.wait_send)
-    for group in (s00, s01, s10, s11, o00, o01, o10, o11, u0, u1):
-        for cp in group.values():
-            cp.wait_send()
+    for group in (s00, s01, s10, s11, o00, o01, o10, o11, u0, u1, u2, u3):
+        for cond, cp in group.values():
+            when(cond, cp.wait_send)
     for cp in (c00, c01, c10, c11):
         cp.wait_send()
-    for to, cp in away.values():
-        @pl.when(to != z)
-        def _():
-            cp.wait_send()
+    for group in away.values():
+        for cond, cp in group:
+            when(cond, cp.wait_send)
 
 
 def local(hamiltonian, h_mask, factor, z_mask, k_mask, block_sizes):
@@ -350,14 +426,15 @@
         pltpu.VMEM((2, CHUNKS, 256, 256), F32),
         pltpu.VMEM((2, CHUNKS, 3, HALF, 256), F32),
         pltpu.VMEM((CHUNKS, 2, 2, 256, 256), F32),
-        pltpu.VMEM((CHUNKS, 4, HALF, 512), F32),
-        pltpu.VMEM((CHUNKS, 3, HALF, 512), F32),
-        pltpu.VMEM((CHUNKS, 4, HALF, B), F32),
-        pltpu.VMEM((4, CHUNKS, HALF, B), F32),
+        pltpu.VMEM((512, 1024), bf), pltpu.VMEM((512, 1024), bf),
+        pltpu.VMEM((4, 4, B, B), F32),
+        pltpu.VMEM((4, 3, B, B), F32),
+        pltpu.VMEM((4, B, B), F32), pltpu.VMEM((4, B, B), F32),
+        pltpu.VMEM((4, B, B), F32),
         dma((2, 4, 4)), dma((2, 4, 4)), dma((2, 4, 4)), dma((2, 4, 4)),
         dma((2,)), dma((4, 2)), dma((4, 2)),
         dma((2, 2)), dma((2, 2)), dma((2, 2, 4)), dma((2, 2, 4)), dma((2, 2, 4)), dma((2, 2, 4)),
-        dma((2, 2, 4)), dma((2, 2, 4)), dma((2, 4)), dma((2, 4)), dma((2, 4)), dma((2, 4)),
+        dma((2, 2, 4)), dma((2, 2, 4)), dma((4, 4)), dma((4, 4)), dma((4,)), dma((4,)), dma((4,)),
     ]
     hbm = pl.BlockSpec(memory_space=pltpu.HBM)
     return pl.pallas_call(

time: 85.9 us -> 82.2 us (0.957)
  Pallas kernels: 83.5 us -> 80.5 us
    pallas_call x1, Pallas kernels: 83.5 us -> 80.5 us  [local(): pl.pallas_call(kernel, out_shape=jax.ShapeDtypeStruct((512, B), F32), in_...]
where the time goes in v4:
time: 82.2 us; the launch traced here: 81.2 us
  Pallas kernels  80.5 us (98%)
    pallas_call x1, Pallas kernels, local(): pl.pallas_call(kernel, out_shape=jax.ShapeDtypeStruct((512, B), F32), in_...  80.5 us

profile of v4, /device:TPU:34, one launch (start us, length us, event | category | flops | bytes accessed | tf_op | source)
XLA Modules:
  0.0 81.2 jit_solution(157087665797162584)
XLA Ops:
  0.0 80.5 %congruence.1 = f32[512,128]{1,0:T(8,128)S(1)} custom-call(f32[512,128]{1,0:T(8,128)} %h_hbm.1, s32[1,4]{1,0:T(1,128)} %bitcast.3, f32[512,128]{1,0:T(8,128)} %z_hbm.1, s32[1,4]{1,0:T(1,128)} %bitcast.4, s32[1,4]{1,0:T(1,128)} %bitcast.5, s32[32]{0:T(128)} %size_hbm.1), custom_call_target="tpu_custom_call" | custom-call | tf_op jit(solution)/shard_map/congruence/pallas_call | solution.py:440
  80.5 0.7 copy.8

commit v5 on v3

--- a/solution.py
+++ b/solution.py
@@ -11,11 +11,19 @@
 F32 = jnp.float32
 CHUNKS = 2
 HALF = B // CHUNKS
+OWNER = ((0, 0, 1, 2), (0, 0, 1, 3))
 
 
 def split(v):
     hi = v.astype(jnp.bfloat16)
     return hi, (v - hi.astype(F32)).astype(jnp.bfloat16)
+
+
+def when(cond, act):
+    if cond is None:
+        act()
+    else:
+        pl.when(cond)(act)
 
 
 def dot3(ah, al, bh, bl, axis):
@@ -26,9 +34,9 @@
 
 def kernel(h_hbm, hm_hbm, z_hbm, zm_hbm, km_hbm, size_hbm, out_ref,
            h_ref, z_ref, hm_ref, zm_ref, km_ref, size_ref, in_s,
-           hg, zg, ah, al, bh, bl, sw, z1, z1h, z1l, wp, cr, wc, yr, wt, u, xr, fin, tr,
+           hg, zg, ah, al, bh, bl, sw, z1, z1h, z1l, wp, cr, wc, yr, wt, wh, wl, u, xr, fin, fint, tr,
            h_ss, h_rs, z_ss, z_rs, sw_s, z1_ss, z1_rs,
-           wc_ss, wc_rs, wy_ss, wy_rs, wa_ss, wa_rs, wf_ss, wf_rs, ux_ss, ux_rs, fd_ss, fd_rs):
+           wc_ss, wc_rs, wy_ss, wy_rs, wa_ss, wa_rs, wf_ss, wf_rs, ux_ss, ux_rs, fd_ss, fm_ss, fd_rs):
     row = lax.axis_index("row")
     col = lax.axis_index("col")
     x, zl = row // 2, row % 2
@@ -52,7 +60,7 @@
 
     sib = dev(x, y, z, 1 - c)
     xpeer = [None] + [dev((x + d) % 4, y, z, c) for d in (1, 2, 3)]
-    ypeer = [None] + [dev(x, (y + d) % 4, z, c) for d in (1, 2, 3)]
+    ypeer = [dev(x, (y + d) % 4, z, c) for d in (1, 2, 3)]
     zpeer = [dev(x, y, (z + 1) % 8, c), dev(x, y, (z + 7) % 8, c)]
     partner = dev(x, y, zh * 2 + c, zl)
     crossed = zl != c
@@ -60,15 +68,21 @@
     diag = x == y
 
     barrier = pltpu.get_barrier_semaphore()
-    for to in [sib] + xpeer[1:] + ypeer[1:] + zpeer:
+    for to in [sib] + xpeer[1:] + ypeer + zpeer:
         pl.semaphore_signal(barrier, inc=1, device_id=to, device_id_type=MESH)
 
     @pl.when(crossed)
     def _():
         pl.semaphore_signal(barrier, inc=1, device_id=partner, device_id_type=MESH)
 
+    lower = x >= y
+    for p in range(2):
+        @pl.when(x < y)
+        def _():
+            pl.semaphore_signal(barrier, inc=1, device_id=dev(y, x, 2 * zh + c, p), device_id_type=MESH)
+
     for b in range(4):
-        @pl.when(zl * 4 + b != z)
+        @pl.when(jnp.logical_and(lower, zl * 4 + b != z))
         def _():
             pl.semaphore_signal(barrier, inc=1, device_id=dev(x, y, zl * 4 + b, c), device_id_type=MESH)
 
@@ -90,7 +104,8 @@
         zg[z, s * B:(s + 1) * B, :] = z_ref[b * B:(b + 1) * B, :] * (ok * up * zm_ref[0, b].astype(F32))
         hg[z, s * B:(s + 1) * B, :] = h_ref[b * B:(b + 1) * B, :] * (ok * hm_ref[0, b].astype(F32))
 
-    pl.semaphore_wait(barrier, 21 + crossed.astype(jnp.int32) - homed.astype(jnp.int32) - diag.astype(jnp.int32))
+    greets = jnp.where(lower, 4 - homed.astype(jnp.int32), 0) + jnp.where(x > y, 2, 0)
+    pl.semaphore_wait(barrier, 17 + crossed.astype(jnp.int32) - diag.astype(jnp.int32) + greets)
 
     swap = remote(zg.at[z], sw, sw_s.at[0], sw_s.at[1], partner)
 
@@ -117,8 +132,8 @@
                 cp.start()
                 made[st, s, d] = cp
 
-        def last():
-            for s in range(4):
+        def last(subs):
+            for s in subs:
                 made[3, s, s % 2].wait_recv()
 
         def sent():
@@ -130,12 +145,13 @@
     hstep, hlast, hsent = ring(hg, h_ss, h_rs)
     zstep, zlast, zsent = ring(zg, z_ss, z_rs)
 
-    def parts(buf, hi_ref, lo_ref, dist):
+    def parts(buf, hi_ref, lo_ref, dist, rows=slice(0, 512)):
         for slot in {0: [z], 4: [(z + 4) % 8]}.get(dist, [(z + dist) % 8, (z + 8 - dist) % 8]):
-            hi, lo = split(buf[slot])
-            hi_ref[slot] = hi
-            lo_ref[slot] = lo
-
+            hi, lo = split(buf[slot, rows, :])
+            hi_ref[slot, rows, :] = hi
+            lo_ref[slot, rows, :] = lo
+
+    pair = (slice(0, 256), slice(256, 512))
     for s in range(4):
         hstep(0, s)
     parts(hg, ah, al, 0)
@@ -179,12 +195,14 @@
             z1h[m, q * HALF:(q + 1) * HALF, :] = hi[m * HALF:(m + 1) * HALF, :]
             z1l[m, q * HALF:(q + 1) * HALF, :] = lo[m * HALF:(m + 1) * HALF, :]
 
-    def whole(ref):
-        return jnp.concatenate(
-            [jnp.concatenate([ref[2 * q + half] for q in range(4)], axis=1) for half in range(2)], axis=0)
+    def both(*conds):
+        out = conds[0]
+        for cond in conds[1:]:
+            out = jnp.logical_and(out, cond)
+        return out
 
     kz = [1 - zl, zl]
-    myrow = pl.ds(pl.multiple_of(y * HALF, HALF), HALF)
+    uses = [both(x <= y, y <= q) for q in range(4)]
 
     def first(k, m):
         rh, rl = [jnp.concatenate([ref[2 * q + kz[k]] for q in range(4)], axis=1) for ref in (ah, al)]
@@ -199,114 +217,165 @@
         cp.wait_recv()
         wc[k, m] = wp[k, m, c] + cr[k, m]
         cps = {}
-        for d in (2, 1, 3):
-            piece = pl.ds(pl.multiple_of(((y + d) % 4) * HALF, HALF), HALF)
-            cps[d] = remote(wc.at[k, m, piece], yr.at[k, m, d - 1], wy_ss.at[k, m, d], wy_rs.at[k, m, d], ypeer[d])
-            cps[d].start()
+        for q in (3, 2, 1):
+            for src in range(q + 1):
+                to = OWNER[m][q]
+                if src != to:
+                    cond = both(y == src, x <= q)
+                    cp = remote(wc.at[k, m, pl.ds(q * HALF, HALF)], yr.at[k, m, q, src],
+                                wy_ss.at[k, m, q, src], wy_rs.at[k, m, q, src], dev(x, to, z, c))
+                    cps[q, src] = cond, cp
+                    when(cond, cp.start)
         return cps
 
     def spread(k, m, cps):
-        for d in (1, 3, 2):
-            cps[d].wait_recv()
-        wt[m, kz[k], c, myrow, :] = (wc[k, m, myrow, :] + yr[k, m, 0]) + (yr[k, m, 1] + yr[k, m, 2])
-        own = wt.at[m, kz[k], c, myrow]
         out = {}
-        for d in (2, 1, 3):
-            out[d] = remote(own, own, wa_ss.at[k, m, d], wa_rs.at[k, m, d], ypeer[d])
-            out[d].start()
-        out[0] = remote(own, own, wf_ss.at[k, m, 0], wf_rs.at[k, m, 0], sib)
-        out[0].start()
+        for q in (3, 2, 1, 0):
+            rows = pl.ds(q * HALF, HALF)
+            mine = both(y == OWNER[m][q], x <= q)
+            own = wt.at[m, k, c, rows]
+
+            @pl.when(mine)
+            def _():
+                wt[m, k, c, rows, :] = wc[k, m, rows, :]
+                for src in range(q + 1):
+                    if src != OWNER[m][q]:
+                        cps[q, src][1].wait_recv()
+                        wt[m, k, c, rows, :] += yr[k, m, q, src]
+
+            for to in range(q + 1):
+                if to != OWNER[m][q]:
+                    cond = both(mine, x <= to)
+                    out[q, to] = cond, remote(own, own, wa_ss.at[k, m, q, to], wa_rs.at[k, m, q], dev(x, to, z, c))
+                    when(cond, out[q, to][1].start)
+            out[q, 4] = uses[q], remote(own, own, wf_ss.at[k, m, q], wf_rs.at[k, m, q], sib)
+            when(both(mine, uses[q]), out[q, 4][1].start)
         return out
 
     def forward(k, m, out):
-        for d in (1, 3, 2):
-            out[d].wait_recv()
-            part = wt.at[m, kz[k], c, pl.ds(pl.multiple_of(((y + 4 - d) % 4) * HALF, HALF), HALF)]
-            out[d + 3] = remote(part, part, wf_ss.at[k, m, d], wf_rs.at[k, m, d], sib)
-            out[d + 3].start()
+        for q in (3, 2, 1):
+            @pl.when(both(uses[q], y != OWNER[m][q]))
+            def _():
+                out[q, q if q != OWNER[m][q] else 0][1].wait_recv()
+                out[q, 4][1].start()
+
+    def gathered(k, m, out):
+        for q in range(4):
+            when(uses[q], out[q, 4][1].wait_recv)
+        for half in range(2):
+            hi, lo = split(wt[m, k, half])
+            at = (k * 2 + half) * 256
+            wh[m, :, at:at + 256] = hi
+            wl[m, :, at:at + 256] = lo
+
+    shift = zl * 2 + 3
+    near = [zh, (zh + shift) % 4, (zh + 4 - shift % 4) % 4, (zh + 2) % 4]
+
+    def second(js, m):
+        rh, rl = [
+            jnp.concatenate(
+                [jnp.concatenate([ref[2 * near[j] + kz[k], pair[half], :] for k in range(2) for half in range(2)], axis=0)
+                 for j in js], axis=1)
+            for ref in (bh, bl)]
+        t = dot3(wh[m], wl[m], rh, rl, 0)
+        for i, j in enumerate(js):
+            for q in range(4):
+                u[j, m, q] = t[q * HALF:(q + 1) * HALF, i * B:(i + 1) * B]
+            for d in (2, 1, 3):
+                q = (x + d) % 4
+                cond = jnp.logical_and(x <= y, q >= y)
+                cp = remote(u.at[j, m, q], xr.at[j, m, d - 1], ux_ss.at[j, m, d], ux_rs.at[j, m, d], xpeer[d])
+                scattered[j, m, d] = cond, cp
+                when(cond, cp.start)
+
+    scattered = {}
+    place = (zh % 2) * 2 + zl
+    away = {}
+
+    def deliver(j):
+        for m in range(CHUNKS):
+            rows = slice(m * HALF, (m + 1) * HALF)
+            fin[j, rows, :] = jnp.where(diag, u[j, m, x], 0.0)
+            for d in (1, 3, 2):
+                @pl.when(jnp.logical_and(lower, (x + 4 - d) % 4 <= y))
+                def _():
+                    scattered[j, m, d][1].wait_recv()
+                    fin[j, rows, :] += xr[j, m, d - 1]
+
+        to = 2 * near[j] + zh // 2
+        slot = (near[j] % 2) * 2 + c
+        away[j] = [
+            (jnp.logical_and(lower, to != z),
+             remote(fin.at[j], tr.at[place], fd_ss.at[j], fd_rs.at[place], dev(x, y, to, c))),
+            (x > y,
+             remote(fint.at[j], tr.at[slot], fm_ss.at[j], fd_rs.at[slot], dev(y, x, 2 * zh + near[j] // 2, zl))),
+        ]
+        when(away[j][0][0], away[j][0][1].start)
+
+        @pl.when(x > y)
+        def _():
+            fint[j] = fin[j].T
+            away[j][1][1].start()
+
+        @pl.when(jnp.logical_and(lower, to == z))
+        def _():
+            tr[place] = fin[j]
 
     c00 = first(0, 0)
     c01 = first(0, 1)
-    hlast()
+    s00 = scatter(0, 0, c00)
+    s01 = scatter(0, 1, c01)
+    hlast(range(4))
     parts(hg, ah, al, 4)
-    s00 = scatter(0, 0, c00)
     c10 = first(1, 0)
-    s01 = scatter(0, 1, c01)
     c11 = first(1, 1)
+    zstep(1, 0)
     s10 = scatter(1, 0, c10)
     o00 = spread(0, 0, s00)
     s11 = scatter(1, 1, c11)
-    zstep(1, 0)
+    o01 = spread(0, 1, s01)
     zstep(1, 1)
-    o01 = spread(0, 1, s01)
     zstep(1, 2)
     zstep(1, 3)
     parts(zg, bh, bl, 1)
     forward(0, 0, o00)
+    forward(0, 1, o01)
     o10 = spread(1, 0, s10)
     zstep(2, 0)
     zstep(2, 1)
     o11 = spread(1, 1, s11)
-    forward(0, 1, o01)
+    gathered(0, 0, o00)
+    gathered(0, 1, o01)
     zstep(2, 2)
     zstep(2, 3)
     parts(zg, bh, bl, 2)
+    forward(1, 0, o10)
+    gathered(1, 0, o10)
+    second((0, 1), 0)
+    forward(1, 1, o11)
+    gathered(1, 1, o11)
+    second((0, 1), 1)
     zstep(3, 0)
     zstep(3, 1)
-    forward(1, 0, o10)
     zstep(3, 2)
     zstep(3, 3)
     parts(zg, bh, bl, 3)
-    zlast()
+    second((2,), 0)
+    second((2,), 1)
+    deliver(0)
+    deliver(1)
+    zlast(range(4))
     parts(zg, bh, bl, 4)
-
-    def second(m, outs):
-        for out in outs:
-            for d in (0, 4, 5, 6):
-                out[d].wait_recv()
-        hi, lo = split(jnp.concatenate([wt[m, half, p] for half in range(2) for p in range(2)], axis=1))
-        t = dot3(hi, lo, whole(bh), whole(bl), 0)
-        for q in range(4):
-            u[m, q] = t[q * HALF:(q + 1) * HALF, :]
-        cps = {}
-        for d in (1, 3, 2):
-            cps[d] = remote(u.at[m, (x + d) % 4], xr.at[m, d - 1], ux_ss.at[m, d], ux_rs.at[m, d], xpeer[d])
-            cps[d].start()
-        return cps
-
-    place = (zh % 2) * 2 + zl
-    away = {}
-
-    def deliver(m, cps):
-        for d in (1, 3, 2):
-            cps[d].wait_recv()
-        v = (u[m, x] + xr[m, 0]) + (xr[m, 1] + xr[m, 2])
-        for q in range(4):
-            fin[m, q] = v[:, q * B:(q + 1) * B]
-            to = 2 * q + zh // 2
-            cp = remote(fin.at[m, q], tr.at[place, m], fd_ss.at[m, q], fd_rs.at[m, place], dev(x, y, to, c))
-            away[m, q] = to, cp
-
-            @pl.when(to == z)
-            def _():
-                tr[place, m] = fin[m, q]
-
-            @pl.when(to != z)
-            def _():
-                cp.start()
-
-    u0 = second(0, (o00, o10))
-    forward(1, 1, o11)
-    u1 = second(1, (o01, o11))
-    deliver(0, u0)
-    deliver(1, u1)
-    for m in range(CHUNKS):
-        for b in range(4):
-            @pl.when(zl * 4 + b != z)
-            def _():
-                remote(fin.at[0, 0], tr.at[b, m], fd_ss.at[0, 0], fd_rs.at[m, b], sib).wait_recv()
-
-            out_ref[b * B + m * HALF:b * B + (m + 1) * HALF, :] = tr[b, m] * km_ref[0, b].astype(F32)
+    second((3,), 0)
+    second((3,), 1)
+    deliver(2)
+    deliver(3)
+    for b in range(4):
+        @pl.when(jnp.logical_not(jnp.logical_and(lower, zl * 4 + b == z)))
+        def _():
+            remote(fin.at[0], tr.at[b], fd_ss.at[0], fd_rs.at[b], sib).wait_recv()
+
+        out_ref[b * B:(b + 1) * B, :] = tr[b] * km_ref[0, b].astype(F32)
 
     hsent()
     zsent()
@@ -320,15 +389,14 @@
             cp.wait_send()
         else:
             pl.when(jnp.logical_not(own))(cp.wait_send)
-    for group in (s00, s01, s10, s11, o00, o01, o10, o11, u0, u1):
-        for cp in group.values():
-            cp.wait_send()
+    for group in (s00, s01, s10, s11, o00, o01, o10, o11, scattered):
+        for cond, cp in group.values():
+            when(cond, cp.wait_send)
     for cp in (c00, c01, c10, c11):
         cp.wait_send()
-    for to, cp in away.values():
-        @pl.when(to != z)
-        def _():
-            cp.wait_send()
+    for group in away.values():
+        for cond, cp in group:
+            when(cond, cp.wait_send)
 
 
 def local(hamiltonian, h_mask, factor, z_mask, k_mask, block_sizes):
@@ -348,16 +416,17 @@
         pltpu.VMEM((2, CHUNKS, 2, 256, 256), F32),
         pltpu.VMEM((2, CHUNKS, 256, 256), F32),
         pltpu.VMEM((2, CHUNKS, 256, 256), F32),
-        pltpu.VMEM((2, CHUNKS, 3, HALF, 256), F32),
+        pltpu.VMEM((2, CHUNKS, 4, 4, HALF, 256), F32),
         pltpu.VMEM((CHUNKS, 2, 2, 256, 256), F32),
-        pltpu.VMEM((CHUNKS, 4, HALF, 512), F32),
-        pltpu.VMEM((CHUNKS, 3, HALF, 512), F32),
-        pltpu.VMEM((CHUNKS, 4, HALF, B), F32),
-        pltpu.VMEM((4, CHUNKS, HALF, B), F32),
+        pltpu.VMEM((CHUNKS, 256, 1024), bf), pltpu.VMEM((CHUNKS, 256, 1024), bf),
+        pltpu.VMEM((4, CHUNKS, 4, HALF, B), F32),
+        pltpu.VMEM((4, CHUNKS, 3, HALF, B), F32),
+        pltpu.VMEM((4, B, B), F32), pltpu.VMEM((4, B, B), F32),
+        pltpu.VMEM((4, B, B), F32),
         dma((2, 4, 4)), dma((2, 4, 4)), dma((2, 4, 4)), dma((2, 4, 4)),
         dma((2,)), dma((4, 2)), dma((4, 2)),
-        dma((2, 2)), dma((2, 2)), dma((2, 2, 4)), dma((2, 2, 4)), dma((2, 2, 4)), dma((2, 2, 4)),
-        dma((2, 2, 4)), dma((2, 2, 4)), dma((2, 4)), dma((2, 4)), dma((2, 4)), dma((2, 4)),
+        dma((2, 2)), dma((2, 2)), dma((2, 2, 4, 4)), dma((2, 2, 4, 4)), dma((2, 2, 4, 4)), dma((2, 2, 4)),
+        dma((2, 2, 4)), dma((2, 2, 4)), dma((4, 2, 4)), dma((4, 2, 4)), dma((4,)), dma((4,)), dma((4,)),
     ]
     hbm = pl.BlockSpec(memory_space=pltpu.HBM)
     return pl.pallas_call(

time: 85.9 us -> 76.2 us (0.89); the launches traced: 84.2 us -> 75.7 us
  Pallas kernels: 83.5 us -> 75 us
    pallas_call x1, Pallas kernels: 83.5 us -> 75 us  [local(): pl.pallas_call(kernel, out_shape=jax.ShapeDtypeStruct((512, B), F32), in_...]
where the time goes in v5:
time: 76.2 us; the launch traced here: 75.7 us
  Pallas kernels  75 us (98%)
    pallas_call x1, Pallas kernels, local(): pl.pallas_call(kernel, out_shape=jax.ShapeDtypeStruct((512, B), F32), in_...  75 us

profile of v5, /device:TPU:34, one launch (start us, length us, event | category | flops | bytes accessed | tf_op | source)
XLA Modules:
  0.0 75.7 jit_solution(17631397773804210264)
XLA Ops:
  0.0 75.0 %congruence.1 = f32[512,128]{1,0:T(8,128)S(1)} custom-call(f32[512,128]{1,0:T(8,128)} %h_hbm.1, s32[1,4]{1,0:T(1,128)} %bitcast.3, f32[512,128]{1,0:T(8,128)} %z_hbm.1, s32[1,4]{1,0:T(1,128)} %bitcast.4, s32[1,4]{1,0:T(1,128)} %bitcast.5, s32[32]{0:T(128)} %size_hbm.1), custom_call_target="tpu_custom_call" | custom-call | tf_op jit(solution)/shard_map/congruence/pallas_call | solution.py:432
  75.0 0.7 copy.8

commit v6 on v5

--- a/solution.py
+++ b/solution.py
@@ -328,34 +328,34 @@
     hlast(range(4))
     parts(hg, ah, al, 4)
     c10 = first(1, 0)
+    zstep(1, 0)
     c11 = first(1, 1)
-    zstep(1, 0)
+    zstep(1, 1)
     s10 = scatter(1, 0, c10)
     o00 = spread(0, 0, s00)
     s11 = scatter(1, 1, c11)
     o01 = spread(0, 1, s01)
-    zstep(1, 1)
     zstep(1, 2)
     zstep(1, 3)
     parts(zg, bh, bl, 1)
     forward(0, 0, o00)
-    forward(0, 1, o01)
     o10 = spread(1, 0, s10)
     zstep(2, 0)
+    zstep(2, 2)
+    forward(0, 1, o01)
     zstep(2, 1)
     o11 = spread(1, 1, s11)
     gathered(0, 0, o00)
     gathered(0, 1, o01)
-    zstep(2, 2)
+    forward(1, 0, o10)
+    gathered(1, 0, o10)
     zstep(2, 3)
     parts(zg, bh, bl, 2)
-    forward(1, 0, o10)
-    gathered(1, 0, o10)
     second((0, 1), 0)
     forward(1, 1, o11)
+    zstep(3, 0)
     gathered(1, 1, o11)
     second((0, 1), 1)
-    zstep(3, 0)
     zstep(3, 1)
     zstep(3, 2)
     zstep(3, 3)

time: 76.2 us -> 75.7 us (level)
  no operation moved by 1% of the time
where the time goes in v6:
time: 75.7 us; the launch traced here: 75.6 us
  Pallas kernels  74.8 us (99%)
    pallas_call x1, Pallas kernels, local(): pl.pallas_call(kernel, out_shape=jax.ShapeDtypeStruct((512, B), F32), in_...  74.8 us

profile of v6, /device:TPU:34, one launch (start us, length us, event | category | flops | bytes accessed | tf_op | source)
XLA Modules:
  0.0 75.6 jit_solution(136521848973241688)
XLA Ops:
  0.0 74.8 %congruence.1 = f32[512,128]{1,0:T(8,128)S(1)} custom-call(f32[512,128]{1,0:T(8,128)} %h_hbm.1, s32[1,4]{1,0:T(1,128)} %bitcast.3, f32[512,128]{1,0:T(8,128)} %z_hbm.1, s32[1,4]{1,0:T(1,128)} %bitcast.4, s32[1,4]{1,0:T(1,128)} %bitcast.5, s32[32]{0:T(128)} %size_hbm.1), custom_call_target="tpu_custom_call" | custom-call | tf_op jit(solution)/shard_map/congruence/pallas_call | solution.py:432
  74.9 0.7 copy.8

commit v7 on v6

--- a/solution.py
+++ b/solution.py
@@ -92,7 +92,7 @@
             def _():
                 pl.semaphore_signal(barrier, inc=1, device_id=dev(y, q, z, p), device_id_type=MESH)
 
-    for cp in loads:
+    for cp in loads[:3]:
         cp.wait()
     ri = lax.broadcasted_iota(jnp.int32, (B, B), 0)
     ci = lax.broadcasted_iota(jnp.int32, (B, B), 1)
@@ -102,6 +102,10 @@
         ok = jnp.logical_and(colok, ri < size_ref[rb]).astype(F32)
         up = (ri + rb * B <= ci + col * B).astype(F32)
         zg[z, s * B:(s + 1) * B, :] = z_ref[b * B:(b + 1) * B, :] * (ok * up * zm_ref[0, b].astype(F32))
+    for cp in loads[3:5]:
+        cp.wait()
+    for s, b in enumerate(ORDER):
+        ok = jnp.logical_and(colok, ri < size_ref[row * 4 + b]).astype(F32)
         hg[z, s * B:(s + 1) * B, :] = h_ref[b * B:(b + 1) * B, :] * (ok * hm_ref[0, b].astype(F32))
 
     greets = jnp.where(lower, 4 - homed.astype(jnp.int32), 0) + jnp.where(x > y, 2, 0)
@@ -370,6 +374,7 @@
     second((3,), 1)
     deliver(2)
     deliver(3)
+    loads[5].wait()
     for b in range(4):
         @pl.when(jnp.logical_not(jnp.logical_and(lower, zl * 4 + b == z)))
         def _():

time: 75.7 us -> 75.7 us (level)
  no operation moved by 1% of the time
where the time goes in v7:
time: 75.7 us; the launch traced here: 75.6 us
  Pallas kernels  74.8 us (99%)
    pallas_call x1, Pallas kernels, local(): pl.pallas_call(kernel, out_shape=jax.ShapeDtypeStruct((512, B), F32), in_...  74.8 us

profile of v7, /device:TPU:34, one launch (start us, length us, event | category | flops | bytes accessed | tf_op | source)
XLA Modules:
  0.0 75.6 jit_solution(1212053336535204225)
XLA Ops:
  0.0 74.8 %congruence.1 = f32[512,128]{1,0:T(8,128)S(1)} custom-call(f32[512,128]{1,0:T(8,128)} %h_hbm.1, s32[1,4]{1,0:T(1,128)} %bitcast.3, f32[512,128]{1,0:T(8,128)} %z_hbm.1, s32[1,4]{1,0:T(1,128)} %bitcast.4, s32[1,4]{1,0:T(1,128)} %bitcast.5, s32[32]{0:T(128)} %size_hbm.1), custom_call_target="tpu_custom_call" | custom-call | tf_op jit(solution)/shard_map/congruence/pallas_call | solution.py:437
  74.9 0.7 copy.8
